TPU v7x, 128 devices: a whole 4x4x4 slice. The times are simulated.
128 devices in a mesh: dp: 32 (over x, y, core), seq: 4 (over z).
Axes of the slice: x: 4, y: 4, z: 4, core: 2. Of those that a mesh axis runs over, the one named last changes fastest.
Arguments:
- audio: float32 [32, 655360], P(None, ('dp', 'seq')), may hold values from -0.4 to 0.4
- starts: int32 [32], replicated, may hold values from 0 to 327679, as said below
- lengths: int32 [32], replicated, may hold values from 163840 to 655360, as said below
- slots: int32 [32], replicated, may hold values from 0 to 31, each once
- conv1_weight: bfloat16 [9, 256], replicated, may hold values from -2 to 2
- conv2_weight: bfloat16 [2304, 256], replicated, may hold values from -0.125 to 0.125
- proj_weight: bfloat16 [5120, 1024], P('dp'), may hold values from -0.078125 to 0.078125
- qkv_weight: bfloat16 [1024, 3072], P('dp'), may hold values from -8 to 8
- out_weight: bfloat16 [1024, 1024], P(None, 'dp'), may hold values from -0.1875 to 0.1875
Outputs:
- regrouped: bfloat16 [32, 32, 4, 8, 1024], P('dp', None, 'seq')
- attended: bfloat16 [32, 32, 4, 8, 1024], P('dp', None, 'seq')
Inputs may be any that keep to these rules, and one draw needn't show every extreme that they name: starts plus lengths is at most 655360 for every stream; some stream's utterance covers the whole stream, and some other stream's utterance starts at 327679. `lengths`: some stream's utterance has exactly 163840 samples. `slots`: every row number appears once.
All inputs are finite; a program needn't handle non-finite values.
Results may differ from a plain program's by a relative error of at most 0.013.
Values may be sent and summed in bfloat16 or wider, within the bound.
A program may use at most 128 MiB of HBM per device.

v0:
```python
import functools
import math

import jax
import jax.numpy as jnp
import numpy as np
from jax import lax
from jax.experimental import pallas as pl
from jax.experimental.pallas import tpu as pltpu
from jax.sharding import PartitionSpec as P

D = 1024
HEADS = 8
HEAD_DIM = 128
MELS = 80
N_FFT = 512
HOP = 160
W = 8
CH = 256
ROWS = 32
RIM = 896
SPAN = 5120
EXT = 6272
BF = jnp.bfloat16
F32 = jnp.float32

SAMPLE_RATE = 16000.0
EPS_LOG = 1e-06
EPS_NORM = 1e-05
MASKED = -1e30
VMEM_LIMIT = 62 * 1024 * 1024


def mel_table(size, bands):
    count = size // 2 + 1
    highest = 2595.0 * math.log10(1.0 + SAMPLE_RATE / 1400.0)
    points = np.linspace(0.0, highest, bands + 2)
    edges = 700.0 * (10.0 ** (points / 2595.0) - 1.0)
    edges[0] = 0.0
    edges[-1] = SAMPLE_RATE / 2.0
    frequency = np.arange(count) * (SAMPLE_RATE / size)
    lower = edges[:-2][None, :]
    middle = edges[1:-1][None, :]
    upper = edges[2:][None, :]
    rising = (frequency[:, None] - lower) / (middle - lower)
    falling = (upper - frequency[:, None]) / (upper - middle)
    return np.maximum(0.0, np.minimum(rising, falling)).astype(np.float32)


def split_high_low(table):
    high = np.asarray(table, np.float64).astype(BF)
    low = (np.asarray(table, np.float64) - high.astype(np.float64)).astype(BF)
    return high, low


def spectrum_tables():
    sample = np.arange(N_FFT)
    angle = (sample[:, None] * np.arange(N_FFT // 2)[None, :] % N_FFT) * (2.0 * math.pi / N_FFT)
    window = 0.5 - 0.5 * np.cos(sample * (2.0 * math.pi / N_FFT))
    return split_high_low(np.concatenate([np.cos(angle), np.sin(angle)], axis=1) * window[:, None])


def filter_tables():
    padded = np.zeros((N_FFT // 2, 128), np.float64)
    padded[:, :MELS] = mel_table(N_FFT, MELS)[: N_FFT // 2]
    return split_high_low(padded)


def patch_table():
    table = np.zeros((3 * 128, 40 * 16), np.float32)
    for g in range(40):
        for a in range(3):
            for b in range(3):
                band = 2 * g - 1 + b
                if 0 <= band < MELS:
                    table[a * 128 + band, g * 16 + 3 * a + b] = 1.0
    return table.astype(BF)


def mm(a, b):
    return jnp.dot(a, b, preferred_element_type=F32)


def halves(value):
    high = value.astype(BF)
    return high, (value - high.astype(F32)).astype(BF)


def frame_step(p, ext, frames_high, frames_low):
    window = ext[:, pl.ds(pl.multiple_of(p * 640, 128), 1152)]
    rows = pl.ds(pl.multiple_of(p * 32, 32), 32)
    for q in range(4):
        start = 64 + HOP * q
        base, offset = start // 128 * 128, start % 128
        if offset:
            piece = pltpu.roll(window[:, base : base + 640], 640 - offset, 1)[:, :N_FFT]
        else:
            piece = window[:, base : base + N_FFT]
        high, low = halves(piece)
        frames_high[q, rows, :] = high
        frames_low[q, rows, :] = low


def mel_step(q, frames_high, frames_low, dft_high, dft_low, mel_high, mel_low, log_mel):
    high, low = frames_high[q], frames_low[q]
    spectrum = mm(high, dft_high[...]) + mm(high, dft_low[...]) + mm(low, dft_high[...])
    half = N_FFT // 2
    power = spectrum[:, :half] * spectrum[:, :half] + spectrum[:, half:] * spectrum[:, half:]
    high, low = halves(power)
    mel = mm(high, mel_high[...]) + mm(high, mel_low[...]) + mm(low, mel_high[...])
    log_mel[q] = jnp.log(mel + EPS_LOG).astype(BF)


def make_patches(log_mel, patch_map, patches):
    even = jnp.concatenate([log_mel[0], log_mel[1], log_mel[2]], axis=1)
    patches[:288, :] = mm(even, patch_map[...]).astype(BF)
    odd = jnp.concatenate([log_mel[2, :256], log_mel[3, :256], log_mel[0, 32:]], axis=1)
    patches[288:, :] = mm(odd, patch_map[...]).astype(BF)


def spread_taps(conv1, taps):
    taps[...] = jnp.zeros_like(taps)
    for j in range(8):
        taps[j, 16 * j : 16 * j + 16, :] = conv1[...]


def conv1_step(g, patches, taps, first):
    block, j = g // 8, g % 8
    lanes = pl.ds(pl.multiple_of(block * 128, 128), 128)
    result = mm(patches[:, lanes], taps[j])
    first[:, pl.ds(pl.multiple_of(g * CH + CH, CH), CH)] = jnp.maximum(result, 0.0).astype(BF)


def conv2_step(h, first, conv2, features):
    lanes = pl.ds(pl.multiple_of(h * 512, 512), 768)
    total = mm(first[0:256, lanes], conv2[0:768, :])
    total += mm(first[288:544, lanes], conv2[768:1536, :])
    total += mm(first[32:288, lanes], conv2[1536:2304, :])
    features[:, pl.ds(pl.multiple_of(h * CH, CH), CH)] = jnp.maximum(total, 0.0).astype(BF)


def to_rows(projected, slots_wide):
    out_index = lax.broadcasted_iota(jnp.int32, (256, 256), 0)
    in_index = lax.broadcasted_iota(jnp.int32, (256, 256), 1)
    same_row = slots_wide == out_index // 8
    same_frame = in_index // 32 == out_index % 8
    routing = jnp.where(same_row & same_frame, 1.0, 0.0).astype(BF)
    return mm(routing, projected).astype(BF)


def front_kernel(
    audio, rim, slots_wide, dft_high, dft_low, mel_high, mel_low, patch_map, conv1, conv2, proj,
    out, ext, frames_high, frames_low, log_mel, patches, taps, first, features,
):
    ext[:, :RIM] = rim[...]
    ext[:, RIM : RIM + SPAN] = audio[...]
    ext[:, RIM + SPAN :] = jnp.zeros((ROWS, EXT - RIM - SPAN), F32)
    spread_taps(conv1, taps)
    first[:, :CH] = jnp.zeros((544, CH), BF)

    @pl.loop(0, 9)
    def _(p):
        frame_step(p, ext, frames_high, frames_low)

    @pl.loop(0, 4)
    def _(q):
        mel_step(q, frames_high, frames_low, dft_high, dft_low, mel_high, mel_low, log_mel)

    make_patches(log_mel, patch_map, patches)

    @pl.loop(0, 40)
    def _(g):
        conv1_step(g, patches, taps, first)

    @pl.loop(0, 20)
    def _(h):
        conv2_step(h, first, conv2, features)

    projected = mm(features[...], proj[...]).astype(BF)
    out[...] = to_rows(projected, slots_wide[...])


def front(audio, rim, slots, conv1_weight, conv2_weight, proj):
    dft_high, dft_low = spectrum_tables()
    mel_high, mel_low = filter_tables()
    args = (
        audio, rim, jnp.tile(slots, 8).reshape(1, 256), dft_high, dft_low, mel_high, mel_low,
        patch_table(), jnp.pad(conv1_weight, ((0, 7), (0, 0))), conv2_weight, proj,
    )
    return pl.pallas_call(
        front_kernel,
        out_shape=jax.ShapeDtypeStruct((256, D), BF),
        in_specs=[pl.BlockSpec(memory_space=pltpu.VMEM)] * len(args),
        out_specs=pl.BlockSpec(memory_space=pltpu.VMEM),
        scratch_shapes=[
            pltpu.VMEM((ROWS, EXT), F32),
            pltpu.VMEM((4, 288, N_FFT), BF),
            pltpu.VMEM((4, 288, N_FFT), BF),
            pltpu.VMEM((4, 288, 128), BF),
            pltpu.VMEM((544, 640), BF),
            pltpu.VMEM((8, 128, CH), BF),
            pltpu.VMEM((544, 41 * CH), BF),
            pltpu.VMEM((256, 20 * CH), BF),
        ],
        compiler_params=pltpu.CompilerParams(vmem_limit_bytes=VMEM_LIMIT),
        name="front",
    )(*args)


def passed_along(block, axis, distance):
    devices = range(lax.axis_size(axis))
    route = [(i - distance, i) for i in devices if i - distance in devices]
    return lax.ppermute(block, axis, route)


def layer_norm(rows):
    values = rows.astype(F32)
    mean = jnp.mean(values, axis=-1, keepdims=True)
    centered = values - mean
    variance = jnp.mean(centered * centered, axis=-1, keepdims=True)
    return (centered * lax.rsqrt(variance + EPS_NORM)).astype(BF)


def frame_mask(begin, span, owners, group, blocks):
    block = jnp.arange(blocks, dtype=jnp.int32)
    offset = jnp.arange(W, dtype=jnp.int32)
    frame = (block[None, :, None] * group + owners[:, None, None]) * W + offset[None, None, :]
    sample = frame * (4 * HOP)
    return ((sample >= begin) & (sample < begin + span)).reshape(-1)


def on_device(
    audio, starts, lengths, slots, conv1_weight, conv2_weight, proj_weight, qkv_weight, out_weight
):
    streams = audio.shape[0]
    rim = passed_along(audio[:, SPAN - RIM :], ("dp", "seq"), 1)
    proj = lax.all_gather(proj_weight, "dp", axis=0, tiled=True)
    ordered = front(audio, rim, slots, conv1_weight, conv2_weight, proj).reshape(streams, W, D)
    received = lax.all_to_all(ordered, "dp", split_axis=0, concat_axis=0, tiled=True)
    rows_here = received.reshape(streams * W, D)
    local_count = rows_here.shape[0]
    mine = lax.axis_index("dp")
    group = lax.axis_size("seq")
    owner = lax.axis_index("seq")
    chosen = slots == mine
    begin = jnp.sum(jnp.where(chosen, starts, 0))
    span = jnp.sum(jnp.where(chosen, lengths, 0))
    valid = frame_mask(begin, span, jnp.reshape(owner, (1,)), group, streams)
    normed = layer_norm(rows_here)
    scale = HEAD_DIM ** (-0.5)
    weights_mix, weights_out = (
        lax.all_gather(qkv_weight, "dp", axis=0, tiled=True),
        lax.all_gather(out_weight, "dp", axis=1, tiled=True),
    )
    mixed = jnp.dot(normed, weights_mix, preferred_element_type=F32).astype(BF)
    queries = mixed[:, :D].reshape(local_count, HEADS, HEAD_DIM)
    key_piece = lax.all_gather(mixed[:, D:].reshape(1, local_count, 2 * D), "seq", axis=0, tiled=True)
    number = key_piece.shape[0]
    key_rows = key_piece[:, :, :D].reshape(number * local_count, HEADS, HEAD_DIM)
    value_rows = key_piece[:, :, D:].reshape(number * local_count, HEADS, HEAD_DIM)
    owners = jnp.arange(number, dtype=jnp.int32)
    key_valid = frame_mask(begin, span, owners, group, streams)
    scores = jnp.einsum("qhd,khd->hqk", queries, key_rows, preferred_element_type=F32) * scale
    masked = jnp.where(key_valid[None, None, :], scores, MASKED)
    peak = jnp.max(masked, axis=2)
    weights = jnp.where(key_valid[None, None, :], jnp.exp(masked - peak[:, :, None]), 0.0)
    total = jnp.sum(weights, axis=2)
    update = jnp.einsum("hqk,khd->hqd", weights.astype(BF), value_rows, preferred_element_type=F32)
    context = (update / total[:, :, None]).transpose(1, 0, 2).reshape(local_count, D).astype(BF)
    output = jnp.dot(context, weights_out, preferred_element_type=F32)
    regrouped = jnp.where(valid[:, None], rows_here, jnp.zeros_like(rows_here))
    attended = jnp.where(valid[:, None], output, 0.0).astype(BF)
    return regrouped.reshape(1, streams, 1, W, D), attended.reshape(1, streams, 1, W, D)


def solution(mesh):
    in_specs = (
        P(None, ("dp", "seq")), P(), P(), P(), P(), P(), P("dp", None), P("dp", None), P(None, "dp"),
    )
    out_specs = (P("dp", None, "seq", None, None), P("dp", None, "seq", None, None))
    return jax.shard_map(
        on_device, mesh=mesh, in_specs=in_specs, out_specs=out_specs, check_vma=False
    )
```

profile of v0, /device:TPU:1, one launch (start us, length us, event | category | flops | bytes accessed | tf_op | source)
XLA Modules:
  0.0 236.2 jit_solution(2016833343732441619)
XLA Ops:
  7.2 0.0 all-gather.6.cloned.1.call-start
  7.2 0.7 all-gather.6.cloned.1.call-update
  7.9 0.0 all-gather.8.cloned.1.call-start
  7.9 0.7 all-gather.8.cloned.1.call-update
  8.6 0.0 all-gather.12.cloned.1.call-start
  8.7 0.9 slice.15
  9.6 4.4 %collective-permute-start = (f32[32,896]{1,0:T(8,128)S(1)}, f32[32,896]{1,0:T(8,128)S(1)}, u32[]{:S(2)}, u32[]{:S(2)}) collective-permute-start(f32[32,896]{1,0:T(8,128)S(1)} %slice.15), channel_id=1, source_target_pairs={{0,1},{1,2},{2,3},{3,4},{4,5},{5,6},{6,7},{7,8},{8,9},{9,10},{10,1... | collective-permute-start | bytes 344072 | tf_op jit(solution)/shard_map/ppermute | solution.py:213
  14.0 0.7 tile.2
  14.6 0.6 reshape_tile.3.slots_wide
  15.3 1.3 pad.4.conv1
  16.6 2.5 %collective-permute-done.rim = f32[32,896]{1,0:T(8,128)S(1)} collective-permute-done((f32[32,896]{1,0:T(8,128)S(1)}, f32[32,896]{1,0:T(8,128)S(1)}, u32[]{:S(2)}, u32[]{:S(2)}) %collective-permute-start) | collective-permute-done | bytes 114720 | tf_op jit(solution)/shard_map/ppermute | solution.py:213
  19.1 0.0 copy-start
  19.1 52.3 %all-gather.6.cloned.1.call-done.proj = bf16[5120,1024]{1,0:T(8,128)(2,1)} async-done(((bf16[160,1024]{1,0:T(8,128)(2,1)}), bf16[5120,1024]{1,0:T(8,128)(2,1)}) %all-gather.6.cloned.1.call-update) | async-done | bytes 10485776 | tf_op jit(solution)/shard_map/all_gather | solution.py:237
  71.4 0.0 copy-done
  71.4 32.6 %front.1 = bf16[256,1024]{1,0:T(8,128)(2,1)} custom-call(f32[32,5120]{1,0:T(8,128)} %audio.1, f32[32,896]{1,0:T(8,128)} %copy-done, s32[1,256]{1,0:T(1,128)} %reshape_tile.3.slots_wide, bf16[512,512]{1,0:T(8,128)(2,1)} %constant.46.clone.dft_high, bf16[512,512]{1,0:T(8,128)(2,1)} %constant.47.clone.dft_low, bf16[256,128]{1,0:T(8,128)(2,1)} %constant.48.clone.mel_high, ...), custom_call_target="tpu_custom_call" | custom-call | tf_op jit(solution)/shard_map/front/pallas_call | solution.py:190
  104.0 22.2 %all_to_all.5 = bf16[32,8,1024]{2,1,0:T(8,128)(2,1)S(1)} all-to-all(bf16[32,8,1024]{2,1,0:T(8,128)(2,1)} %bitcast.46), channel_id=1, replica_groups=mesh['dp'=32,'seq'=4] {'dp'}, dimensions={0} | all-to-all | bytes 1048576 | tf_op jit(solution)/shard_map/all_to_all | solution.py:239
  126.2 0.1 convert_reduce_fusion
  126.4 0.1 div.20
  126.5 0.3 fusion.21
  126.8 0.1 rsqrt.12
  126.9 0.0 copy-start.1
  126.9 0.0 copy-start.2
  126.9 0.0 copy-start.3
  126.9 0.7 all-gather.8.cloned.1.call-done
  127.6 4.7 %convolution_convert_fusion = bf16[256,3072]{1,0:T(8,128)(2,1)S(1)} fusion(bf16[1024,3072]{1,0:T(8,128)(2,1)} %all-gather.8.cloned.1.call-done, bf16[32,8,1024]{2,1,0:T(8,128)(2,1)S(1)} %all_to_all.5, f32[256]{0:T(256)S(1)} %rsqrt.12, f32[256]{0:T(256)S(1)} %div.20), kind=kOutput, calls=%fused_computation.9 | convolution fusion | flops 1612447744 | bytes 8390656 | tf_op jit(solution)/shard_map/dot_general | solution.py:255
  132.3 1.1 slice.21
  133.4 0.0 all-gather.12.cloned.1.call-update
  133.4 0.2 all-gather.10.cloned.1.call-start
  133.6 0.3 all-gather.10.cloned.1.call-update
  134.0 0.0 copy-done.1
  134.0 0.0 copy-done.2
  134.0 0.0 copy-done.3
  134.0 0.6 fusion.38
  135.9 0.7 fusion.36
  136.6 0.1 copy.23
  136.7 0.7 fusion.33
  137.4 0.1 and.27
  137.5 0.1 add.115
  137.6 0.1 add.116
  137.7 0.1 add.118
  137.8 0.7 compare_and_fusion
  138.5 0.9 select_bitcast_fusion
  139.4 40.9 %all-gather.12.cloned.1.call-done = bf16[1024,2048]{1,0:T(8,128)(2,1)} async-done(((bf16[256,2048]{1,0:T(8,128)(2,1)}), bf16[1024,2048]{1,0:T(8,128)(2,1)}) %all-gather.12.cloned.1.call-update) | async-done | bytes 4194320 | tf_op jit(solution)/shard_map/all_gather | solution.py:257
  180.2 2.7 %fusion.41 = (bf16[4,256,1024]{2,1,0:T(8,128)(2,1)S(1)}, bf16[4,256,1024]{2,1,0:T(8,128)(2,1)S(1)}) fusion(bf16[4,256,2048]{2,1,0:T(8,128)(2,1)} %bitcast.45), kind=kLoop, calls=%fused_computation.52 | loop fusion | bytes 8388608 | tf_op jit(solution)/shard_map/slice | solution.py:259
  182.9 0.6 copy.31
  183.6 0.6 copy.30
  184.2 1.3 fusion.8
  185.5 4.6 %fusion.42 = (f32[8,256]{1,0:T(8,128)S(1)}, bf16[8,256,1024]{2,1,0:T(8,128)(2,1)}) fusion(f32[8,256,1024]{2,1,0:T(8,128)S(1)} %fusion.8, pred[1024]{0:T(1024)(128)(4,1)S(1)} %and.27), kind=kOutput, calls=%fused_computation.53 | output fusion | flops 16778240 | bytes 12592128 | tf_op jit(solution)/shard_map/sub | solution.py:266
  190.1 3.7 %divide_convert_fusion = bf16[256,8,128]{0,2,1:T(8,128)(2,1)S(1)} fusion(bf16[1024,8,128]{2,1,0:T(8,128)(2,1)S(1)} %bitcast.47, bf16[8,256,1024]{2,1,0:T(8,128)(2,1)} %get-tuple-element.13, f32[256,8]{0,1:T(8,128)S(1)} %bitcast.49), kind=kOutput, calls=%fused_computation.25 | convolution fusion | flops 537395200 | bytes 6823936 | tf_op jit(solution)/shard_map/hqk,khd->hqd/dot_general | solution.py:268
  193.8 32.7 %all-gather.10.cloned.1.call-done = bf16[1024,1024]{0,1:T(8,128)(2,1)} async-done(((bf16[1024,32]{0,1:T(8,128)(2,1)}), bf16[1024,1024]{0,1:T(8,128)(2,1)}) %all-gather.10.cloned.1.call-update) | async-done | bytes 2097168 | tf_op jit(solution)/shard_map/all_gather | solution.py:253
  226.6 3.1 %fusion.16 = bf16[1,32,1,8,1024]{4,3,2,1,0:T(8,128)(2,1)} fusion(bf16[256,1024]{0,1:T(8,128)(2,1)S(1)} %bitcast.48, bf16[1024,1024]{0,1:T(8,128)(2,1)} %all-gather.10.cloned.1.call-done, pred[256]{0:T(512)(128)(4,1)S(1)} %compare_and_fusion), kind=kOutput, calls=%fused_computation.19 | convolution fusion | flops 537395200 | bytes 3145984 | tf_op jit(solution)/shard_map/dot_general | solution.py:270
  (5 shorter events, 0.0 us)
Async XLA Ops:
  7.2 64.2 %all-gather.6.cloned.1.call-start = ((), (), s32[]{:S(2)}) async-start(), calls=%async_computation.1 | async-start | bytes 10813440 | tf_op jit(solution)/shard_map/all_gather | solution.py:237
  7.9 119.7 %all-gather.8.cloned.1.call-start = ((), (), s32[]{:S(2)}) async-start(), calls=%async_computation.2 | async-start | bytes 6488064 | tf_op jit(solution)/shard_map/all_gather | solution.py:252
  8.6 171.6 %all-gather.12.cloned.1.call-start = ((), (), s32[]{:S(2)}) async-start(), calls=%async_computation.4 | async-start | bytes 5242880 | tf_op jit(solution)/shard_map/all_gather | solution.py:257
  9.6 9.5 %collective-permute-start = (f32[32,896]{1,0:T(8,128)S(1)}, f32[32,896]{1,0:T(8,128)S(1)}, u32[]{:S(2)}, u32[]{:S(2)}) collective-permute-start(f32[32,896]{1,0:T(8,128)S(1)} %slice.15), channel_id=1, source_target_pairs={{0,1},{1,2},{2,3},{3,4},{4,5},{5,6},{6,7},{7,8},{8,9},{9,10},{10,1... | collective-permute-start | bytes 344072 | tf_op jit(solution)/shard_map/ppermute | solution.py:213
  19.1 52.3 %copy-start = (f32[32,896]{1,0:T(8,128)}, f32[32,896]{1,0:T(8,128)S(1)}, u32[]{:S(2)}) copy-start(f32[32,896]{1,0:T(8,128)S(1)} %collective-permute-done.rim) | copy-start | bytes 344068
  126.9 7.1 %copy-start.1 = (s32[32]{0:T(128)S(1)}, s32[32]{0:T(128)}, u32[]{:S(2)}) copy-start(s32[32]{0:T(128)} %param.17) | copy-start | bytes 388
  126.9 7.1 %copy-start.2 = (s32[32]{0:T(128)S(1)}, s32[32]{0:T(128)}, u32[]{:S(2)}) copy-start(s32[32]{0:T(128)} %param.16) | copy-start | bytes 388
  126.9 7.1 %copy-start.3 = (s32[32]{0:T(128)S(1)}, s32[32]{0:T(128)}, u32[]{:S(2)}) copy-start(s32[32]{0:T(128)} %param.15) | copy-start | bytes 388
  133.4 93.2 %all-gather.10.cloned.1.call-start = ((), (), s32[]{:S(2)}) async-start(), calls=%async_computation.3 | async-start | bytes 2162688 | tf_op jit(solution)/shard_map/all_gather | solution.py:253
Sparse Core Ops, SparseCore 0:
  10.2 61.1 all-gather.5
  73.7 53.8 all-gather.7
  133.5 46.6 all-gather.11
  182.4 44.1 all-gather.9
where the time goes:
time: 237 us; the launch traced here: 236 us
  waiting for transfers between devices  131 us (55%)
  Pallas kernels  32.6 us (14%)
  blocking collectives  22.2 us (9%)
  between operations  15.2 us (6%)
  matrix products  12.8 us (5%)
  local copies, waits for them, and re-layouts  9.18 us (4%)
  other arithmetic  8.66 us (4%)
  starting transfers between devices  4.69 us (2%)
    all_gather x1, waiting for transfers between devices, on_device(): proj = lax.all_gather(proj_weight, 'dp', axis=0, tiled=True)  52.3 us
    all_gather x1, waiting for transfers between devices, on_device(): lax.all_gather(mixed[:, D:].reshape(1, local_count, 2 * D), 'seq', axis=0...  40.9 us
    all_gather x1, waiting for transfers between devices, on_device(): lax.all_gather(out_weight, 'dp', axis=1, tiled=True)  32.7 us
    pallas_call x1, Pallas kernels, front(): pl.pallas_call(front_kernel, out_shape=jax.ShapeDtypeStruct((256, D), BF)...  32.6 us
    all_to_all x1, blocking collectives, on_device(): lax.all_to_all(ordered, 'dp', split_axis=0, concat_axis=0, tiled=True)  22.2 us
  transfers between devices with their start and end apart: 5, of which 5 were waited for; matrix products, arithmetic and copies ran while one was open for 9% of the time, Pallas kernels for 14%

commit v1 on v0

v1 whole, which is shorter than its diff:
```python
import functools
import math

import jax
import jax.numpy as jnp
import numpy as np
from jax import lax
from jax.experimental import pallas as pl
from jax.experimental.pallas import tpu as pltpu
from jax.sharding import PartitionSpec as P

D = 1024
HEADS = 8
HEAD_DIM = 128
MELS = 80
N_FFT = 512
HOP = 160
W = 8
CH = 256
ROWS = 32
RIM = 896
SPAN = 5120
EXT = 6272
BF = jnp.bfloat16
F32 = jnp.float32

SAMPLE_RATE = 16000.0
EPS_LOG = 1e-06
EPS_NORM = 1e-05
MASKED = -1e30
VMEM_LIMIT = 62 * 1024 * 1024


def mel_table(size, bands):
    count = size // 2 + 1
    highest = 2595.0 * math.log10(1.0 + SAMPLE_RATE / 1400.0)
    points = np.linspace(0.0, highest, bands + 2)
    edges = 700.0 * (10.0 ** (points / 2595.0) - 1.0)
    edges[0] = 0.0
    edges[-1] = SAMPLE_RATE / 2.0
    frequency = np.arange(count) * (SAMPLE_RATE / size)
    lower = edges[:-2][None, :]
    middle = edges[1:-1][None, :]
    upper = edges[2:][None, :]
    rising = (frequency[:, None] - lower) / (middle - lower)
    falling = (upper - frequency[:, None]) / (upper - middle)
    return np.maximum(0.0, np.minimum(rising, falling)).astype(np.float32)


def split_high_low(table):
    high = np.asarray(table, np.float64).astype(BF)
    low = (np.asarray(table, np.float64) - high.astype(np.float64)).astype(BF)
    return high, low


def spectrum_tables():
    sample = np.arange(N_FFT)
    angle = (sample[:, None] * np.arange(N_FFT // 2)[None, :] % N_FFT) * (2.0 * math.pi / N_FFT)
    window = 0.5 - 0.5 * np.cos(sample * (2.0 * math.pi / N_FFT))
    return split_high_low(np.concatenate([np.cos(angle), np.sin(angle)], axis=1) * window[:, None])


def filter_tables():
    padded = np.zeros((N_FFT // 2, 128), np.float64)
    padded[:, :MELS] = mel_table(N_FFT, MELS)[: N_FFT // 2]
    return split_high_low(padded)


def patch_table():
    table = np.zeros((3 * 128, 40 * 16), np.float32)
    for g in range(40):
        for a in range(3):
            for b in range(3):
                band = 2 * g - 1 + b
                if 0 <= band < MELS:
                    table[a * 128 + band, g * 16 + 3 * a + b] = 1.0
    return table.astype(BF)


def mm(a, b):
    return jnp.dot(a, b, preferred_element_type=F32)


def halves(value):
    high = value.astype(BF)
    return high, (value - high.astype(F32)).astype(BF)


def frame_step(p, ext, frames_high, frames_low):
    window = ext[:, pl.ds(pl.multiple_of(p * 640, 128), 1152)]
    rows = pl.ds(pl.multiple_of(p * 32, 32), 32)
    for q in range(4):
        start = 64 + HOP * q
        base, offset = start // 128 * 128, start % 128
        if offset:
            piece = pltpu.roll(window[:, base : base + 640], 640 - offset, 1)[:, :N_FFT]
        else:
            piece = window[:, base : base + N_FFT]
        high, low = halves(piece)
        frames_high[q, rows, :] = high
        frames_low[q, rows, :] = low


def mel_step(q, frames_high, frames_low, dft_high, dft_low, mel_high, mel_low, log_mel):
    high, low = frames_high[q], frames_low[q]
    spectrum = mm(high, dft_high[...]) + mm(high, dft_low[...]) + mm(low, dft_high[...])
    half = N_FFT // 2
    power = spectrum[:, :half] * spectrum[:, :half] + spectrum[:, half:] * spectrum[:, half:]
    high, low = halves(power)
    mel = mm(high, mel_high[...]) + mm(high, mel_low[...]) + mm(low, mel_high[...])
    log_mel[q] = jnp.log(mel + EPS_LOG).astype(BF)


def make_patches(log_mel, patch_map, patches):
    even = jnp.concatenate([log_mel[0], log_mel[1], log_mel[2]], axis=1)
    patches[:288, :] = mm(even, patch_map[...]).astype(BF)
    odd = jnp.concatenate([log_mel[2, :256], log_mel[3, :256], log_mel[0, 32:]], axis=1)
    patches[288:, :] = mm(odd, patch_map[...]).astype(BF)


def spread_taps(conv1, taps):
    taps[...] = jnp.zeros_like(taps)
    for j in range(8):
        taps[j, 16 * j : 16 * j + 16, :] = conv1[...]


def conv1_step(g, patches, taps, first):
    block, j = g // 8, g % 8
    lanes = pl.ds(pl.multiple_of(block * 128, 128), 128)
    result = mm(patches[:, lanes], taps[j])
    first[:, pl.ds(pl.multiple_of(g * CH + CH, CH), CH)] = jnp.maximum(result, 0.0).astype(BF)


def conv2_step(h, first, conv2, features):
    lanes = pl.ds(pl.multiple_of(h * 512, 512), 768)
    total = mm(first[0:256, lanes], conv2[0:768, :])
    total += mm(first[288:544, lanes], conv2[768:1536, :])
    total += mm(first[32:288, lanes], conv2[1536:2304, :])
    features[:, pl.ds(pl.multiple_of(h * CH, CH), CH)] = jnp.maximum(total, 0.0).astype(BF)


def to_rows(projected, slots_wide):
    out_index = lax.broadcasted_iota(jnp.int32, (256, 256), 0)
    in_index = lax.broadcasted_iota(jnp.int32, (256, 256), 1)
    same_row = slots_wide == out_index // 8
    same_frame = in_index // 32 == out_index % 8
    routing = jnp.where(same_row & same_frame, 1.0, 0.0).astype(BF)
    return mm(routing, projected).astype(BF)

MESH_ID = pl.DeviceIdType.MESH
PART = 2 * HEAD_DIM
WIDE = 3 * PART + D


class Ring:
    def __init__(self, source, buffer, send, recv, place):
        self.source, self.buffer, self.send, self.recv = source, buffer, send, recv
        self.core, self.a, self.b, self.sa, self.sb, self.sibling = place
        self.count = 0
        self.sent = []
        self.rows = buffer.shape[1]

    def shard(self, da, db):
        return lax.rem(self.a + da + 4, 4) * self.sa + lax.rem(self.b + db + 4, 4) * self.sb + self.core

    def part(self, index, half):
        if half is None:
            return self.buffer.at[index]
        step = self.rows // 2
        return self.buffer.at[index, pl.ds(half * step, step)]

    def put(self, index, half, target, slot, own=False):
        copy = pltpu.make_async_remote_copy(
            src_ref=self.source if own else self.part(index, half),
            dst_ref=self.part(index, half),
            send_sem=self.send.at[self.count],
            recv_sem=self.recv.at[slot],
            device_id={"dp": target},
            device_id_type=MESH_ID,
        )
        copy.start()
        self.count += 1
        self.sent.append(copy)

    def got(self, index, half, slot):
        pltpu.make_async_remote_copy(
            src_ref=self.part(index, half),
            dst_ref=self.part(index, half),
            send_sem=self.send.at[0],
            recv_sem=self.recv.at[slot],
            device_id={"dp": self.sibling},
            device_id_type=MESH_ID,
        ).wait_recv()

    def to_b(self, da, own=False):
        index = self.shard(da, 0)
        base = 4 + 4 * (da + 1)
        self.put(index, None, self.shard(0, 1), base, own)
        self.put(index, None, self.shard(0, -1), base + 1, own)
        self.put(index, None, self.sibling, 20 + 4 * (da + 1) + 1, own)

    def begin(self):
        index = self.shard(0, 0)
        self.put(index, None, self.shard(1, 0), 0, True)
        self.put(index, None, self.shard(-1, 0), 1, True)
        self.to_b(0, True)

    def pass_a(self):
        for da, half, slot in ((-1, 0, 0), (1, 1, 1)):
            index = self.shard(da, 0)
            self.got(index, None, slot)
            self.put(index, half, self.shard(-da, 0), 2 + slot)
            self.to_b(da)

    def end_a(self):
        index = self.shard(2, 0)
        self.got(index, 0, 2)
        self.got(index, 1, 3)
        self.to_b(2)

    def pass_b(self, da):
        base = 4 + 4 * (da + 1)
        for db, half, slot in ((-1, 0, 0), (1, 1, 1)):
            index = self.shard(da, db)
            self.got(index, None, base + slot)
            self.put(index, half, self.shard(0, -db), base + 2 + slot)
            self.put(index, None, self.sibling, 20 + 4 * (da + 1) + db + 1)

    def end_b(self, da):
        base = 4 + 4 * (da + 1)
        index = self.shard(da, 2)
        self.got(index, 0, base + 2)
        self.got(index, 1, base + 3)
        self.put(index, None, self.sibling, 20 + 4 * (da + 1) + 3)

    def from_sibling(self):
        for slot in range(16):
            self.got(self.sibling, None, 20 + slot)

    def drain(self):
        for copy in self.sent:
            copy.wait_send()


def normalised(values):
    mean = jnp.mean(values, axis=-1, keepdims=True)
    centered = values - mean
    variance = jnp.mean(centered * centered, axis=-1, keepdims=True)
    return (centered * lax.rsqrt(variance + EPS_NORM)).astype(BF)


def nt(a, b):
    return lax.dot_general(a, b, (((1,), (1,)), ((), ())), preferred_element_type=F32)


def whole_kernel(
    audio_in, starts, lengths, slots, conv1_in, conv2_in, proj_in, qkv_in, out_in,
    dft_high_in, dft_low_in, mel_high_in, mel_low_in, patch_in,
    regrouped, attended,
    ext, frames_high, frames_low, log_mel, patches, taps, first, features,
    conv2, dft_high, dft_low, mel_high, mel_low, patch_map,
    proj, wide, rows_out, rows_all, mixed, context_out, context_in,
    local_sem, halo_sem, proj_send, proj_recv, wide_send, wide_recv,
    row_send, row_recv, z_send, z_recv, context_send, context_recv,
):
    me, z = lax.axis_index("dp"), lax.axis_index("seq")
    x, y, core = me // 8, me // 2 % 4, me % 2
    sibling = me + 1 - 2 * core
    a, b = x * (1 - core) + y * core, y * (1 - core) + x * core
    sa, sb = 8 * (1 - core) + 2 * core, 2 * (1 - core) + 8 * core
    place = (core, a, b, sa, sb, sibling)
    line = me * 4 + z
    after, before = lax.rem(line + 1, 128), lax.rem(line + 127, 128)
    up, down = lax.rem(z + 1, 4), lax.rem(z + 3, 4)

    def local(source, target, index):
        copy = pltpu.make_async_copy(source, target, local_sem.at[index])
        copy.start()
        return copy

    loads = [
        local(source, target, index)
        for index, (source, target) in enumerate(
            (
                (audio_in, ext.at[:, pl.ds(RIM, SPAN)]),
                (dft_high_in, dft_high),
                (dft_low_in, dft_low),
                (mel_high_in, mel_high),
                (mel_low_in, mel_low),
                (patch_in, patch_map),
                (conv2_in, conv2),
                (proj_in, proj.at[me]),
            )
        )
    ]
    parts = [
        local(
            qkv_in.at[:, pl.ds(pl.multiple_of(third * D + z * PART, 128), PART)],
            wide.at[me, :, pl.ds(third * PART, PART)],
            8 + third,
        )
        for third in range(3)
    ]

    barrier = pltpu.get_barrier_semaphore()

    @pl.loop(1, 32)
    def _(offset):
        pl.semaphore_signal(
            barrier, inc=1, device_id={"dp": lax.rem(me + offset, 32)}, device_id_type=MESH_ID
        )

    for offset in range(1, 4):
        pl.semaphore_signal(
            barrier, inc=1, device_id={"seq": lax.rem(z + offset, 4)}, device_id_type=MESH_ID
        )
    for other in (after, before):
        pl.semaphore_signal(
            barrier, inc=1, device_id={"dp": other // 4, "seq": other % 4}, device_id_type=MESH_ID
        )
    spread_taps(conv1_in, taps)
    first[:, :CH] = jnp.zeros((544, CH), BF)
    ext[:, RIM + SPAN :] = jnp.zeros((ROWS, EXT - RIM - SPAN), F32)
    turn = jnp.where(
        lax.broadcasted_iota(jnp.int32, (32, 32), 0) == lax.broadcasted_iota(jnp.int32, (32, 32), 1), 1.0, 0.0
    ).astype(BF)
    wide[me, :, 3 * PART :] = nt(turn, out_in[...]).astype(BF)
    pl.semaphore_wait(barrier, 36)

    halo = pltpu.make_async_remote_copy(
        src_ref=audio_in.at[:, pl.ds(SPAN - RIM, RIM)],
        dst_ref=ext.at[:, pl.ds(0, RIM)],
        send_sem=halo_sem.at[0],
        recv_sem=halo_sem.at[1],
        device_id={"dp": after // 4, "seq": after % 4},
        device_id_type=MESH_ID,
    )
    halo.start()
    ring = Ring(proj_in, proj, proj_send, proj_recv, place)
    ring.begin()

    loads[0].wait()
    halo.wait_recv()

    @pl.when(line == 0)
    def _():
        ext[:, :RIM] = jnp.zeros((ROWS, RIM), F32)

    @pl.loop(0, 9)
    def _(p):
        frame_step(p, ext, frames_high, frames_low)

    for load in loads[1:5]:
        load.wait()

    @pl.loop(0, 4)
    def _(q):
        mel_step(q, frames_high, frames_low, dft_high, dft_low, mel_high, mel_low, log_mel)

    loads[5].wait()
    make_patches(log_mel, patch_map, patches)

    def conv1_run(low, high):
        @pl.loop(low, high)
        def _(g):
            conv1_step(g, patches, taps, first)

    def conv2_run(low, high):
        @pl.loop(low, high)
        def _(h):
            conv2_step(h, first, conv2, features)

    conv1_run(0, 8)
    ring.pass_a()
    conv1_run(8, 16)
    ring.pass_b(0)
    conv1_run(16, 32)
    ring.end_a()
    conv1_run(32, 40)
    loads[6].wait()
    conv2_run(0, 4)
    ring.pass_b(-1)
    conv2_run(4, 8)
    ring.end_b(0)
    ring.pass_b(1)
    conv2_run(8, 12)
    conv2_run(12, 16)
    ring.pass_b(2)
    ring.end_b(-1)
    conv2_run(16, 20)
    ring.end_b(1)
    ring.end_b(2)
    ring.from_sibling()
    loads[7].wait()

    projected = mm(features[...], proj[...].reshape(20 * CH, D)).astype(BF)
    tile_map = jnp.where(
        lax.broadcasted_iota(jnp.int32, (32, 256), 1) % 32 == lax.broadcasted_iota(jnp.int32, (32, 256), 0),
        1.0, 0.0,
    ).astype(BF)
    slot_values = jnp.broadcast_to(slots[...].astype(F32), (8, 32)).astype(BF)
    slots_wide = mm(slot_values, tile_map)[0:1, :].astype(jnp.int32)
    out_index = lax.broadcasted_iota(jnp.int32, (256, 256), 0)
    in_index = lax.broadcasted_iota(jnp.int32, (256, 256), 1)
    routing = jnp.where((slots_wide == out_index // 8) & (in_index // 32 == out_index % 8), 1.0, 0.0).astype(BF)
    rows_out[...] = mm(routing, projected).reshape(32, 8, D).astype(BF)

    def row_copy(offset):
        target = lax.rem(me + offset, 32)
        return pltpu.make_async_remote_copy(
            src_ref=rows_out.at[target],
            dst_ref=rows_all.at[z, me],
            send_sem=row_send.at[offset],
            recv_sem=row_recv.at[me],
            device_id={"dp": target},
            device_id_type=MESH_ID,
        )

    @pl.loop(1, 32)
    def _(offset):
        row_copy(offset).start()

    mine = local(rows_out.at[me], rows_all.at[z, me], 11)
    for part in parts:
        part.wait()
    wide_ring = Ring(wide.at[me], wide, wide_send, wide_recv, place)
    wide_ring.begin()
    mine.wait()

    def z_copy(origin, chunk, upwards, index):
        block = rows_all.at[origin, pl.ds(pl.multiple_of(chunk * 8, 8), 8)]
        return pltpu.make_async_remote_copy(
            src_ref=block,
            dst_ref=block,
            send_sem=z_send.at[index],
            recv_sem=z_recv.at[index],
            device_id={"seq": up if upwards else down},
            device_id_type=MESH_ID,
        )

    z_copies = []
    chunks = [lax.rem(x + index, 4) for index in range(4)]
    for index in range(4):
        @pl.loop(0, 8)
        def _(step):
            source = chunks[index] * 8 + step

            @pl.when(source != me)
            def _():
                block = rows_all.at[z, source]
                pltpu.make_async_remote_copy(
                    src_ref=block,
                    dst_ref=block,
                    send_sem=row_send.at[0],
                    recv_sem=row_recv.at[source],
                    device_id={"dp": sibling},
                    device_id_type=MESH_ID,
                ).wait_recv()

        for direction in range(2):
            copy = z_copy(z, chunks[index], direction == 0, 6 * direction + index)
            copy.start()
            z_copies.append(copy)

    def z_wait(origin, chunk, index):
        z_copy(origin, chunk, True, index).wait_recv()

    def z_forward(index):
        z_wait(down, chunks[index], index)
        z_wait(up, chunks[index], 6 + index)
        if index < 2:
            copy = z_copy(down, chunks[index], True, 4 + index)
        else:
            copy = z_copy(up, chunks[index], False, 6 + 2 + index)
        copy.start()
        z_copies.append(copy)

    wide_ring.pass_a()
    z_forward(0)
    wide_ring.pass_b(0)
    wide_ring.end_a()
    z_forward(1)
    wide_ring.end_b(0)
    wide_ring.pass_b(-1)
    wide_ring.pass_b(1)
    z_forward(2)
    wide_ring.pass_b(2)
    wide_ring.end_b(-1)
    wide_ring.end_b(1)
    wide_ring.end_b(2)
    z_forward(3)
    wide_ring.from_sibling()

    def mix(origin):
        values = rows_all[origin].astype(F32).reshape(256, D)
        result = mm(normalised(values), wide[:, :, : 3 * PART].reshape(D, 3 * PART))
        mixed[pl.ds(pl.multiple_of(origin * 256, 256), 256), :] = result.astype(BF)

    mix(z)
    mix(down)
    mix(up)
    opposite = lax.rem(z + 2, 4)
    for index in range(2):
        z_wait(opposite, chunks[index], 4 + index)
        z_wait(opposite, chunks[2 + index], 6 + 4 + index)
    mix(opposite)

    chosen = slots[...] == me
    begin = jnp.sum(jnp.where(chosen, starts[...].astype(F32), 0.0), axis=1, keepdims=True)
    span = jnp.sum(jnp.where(chosen, lengths[...].astype(F32), 0.0), axis=1, keepdims=True)

    def valid_of(owner, index):
        frame = (index // 8 * 4 + owner) * 8 + index % 8
        sample = (frame * (4 * HOP)).astype(F32)
        return (sample >= begin) & (sample < begin + span)

    key_index = lax.broadcasted_iota(jnp.int32, (1, 1024), 1)
    key_valid = valid_of(key_index // 256, key_index % 256)
    scale = HEAD_DIM ** (-0.5)

    def context_copy(step):
        target = lax.rem(z + 3 - step, 4)
        return pltpu.make_async_remote_copy(
            src_ref=context_out.at[target],
            dst_ref=context_in.at[z],
            send_sem=context_send.at[step],
            recv_sem=context_recv.at[z],
            device_id={"seq": target},
            device_id_type=MESH_ID,
        )

    @pl.loop(0, 4)
    def _(step):
        target = lax.rem(z + 3 - step, 4)
        rows = pl.ds(pl.multiple_of(target * 256, 256), 256)
        for head in range(2):
            lanes = slice(head * HEAD_DIM, (head + 1) * HEAD_DIM)
            query = mixed[rows, lanes]
            key = mixed[:, PART + head * HEAD_DIM : PART + (head + 1) * HEAD_DIM]
            value = mixed[:, 2 * PART + head * HEAD_DIM : 2 * PART + (head + 1) * HEAD_DIM]
            masked = jnp.where(key_valid, nt(query, key) * scale, MASKED)
            weights = jnp.where(
                key_valid, jnp.exp(masked - jnp.max(masked, axis=1, keepdims=True)), 0.0
            )
            total = jnp.sum(weights, axis=1, keepdims=True)
            context_out[target, :, lanes] = (mm(weights.astype(BF), value) / total).astype(BF)

        @pl.when(step < 3)
        def _():
            context_copy(step).start()

    context_in[z] = context_out[z]
    for offset in range(1, 4):
        other = lax.rem(z + offset, 4)
        pltpu.make_async_remote_copy(
            src_ref=context_in.at[other],
            dst_ref=context_in.at[other],
            send_sem=context_send.at[3],
            recv_sem=context_recv.at[other],
            device_id={"seq": up},
            device_id_type=MESH_ID,
        ).wait_recv()

    output = jnp.zeros((256, D), F32)
    for part in range(4):
        start = 3 * PART + part * PART
        output += nt(context_in[part], wide[:, :, start : start + PART].reshape(D, PART))
    row_valid = valid_of(z, lax.broadcasted_iota(jnp.int32, (256, 1), 0))
    attended[...] = jnp.where(row_valid, output, 0.0).reshape(32, 8, D).astype(BF)
    own = rows_all[z].astype(F32).reshape(256, D)
    regrouped[...] = jnp.where(row_valid, own, 0.0).reshape(32, 8, D).astype(BF)

    halo.wait_send()
    ring.drain()
    wide_ring.drain()

    @pl.loop(1, 32)
    def _(offset):
        row_copy(offset).wait_send()

    for copy in z_copies:
        copy.wait_send()

    @pl.loop(0, 3)
    def _(step):
        context_copy(step).wait_send()


def on_device(
    audio, starts, lengths, slots, conv1_weight, conv2_weight, proj_weight, qkv_weight, out_weight
):
    args = (
        audio, starts.reshape(1, 32), lengths.reshape(1, 32), slots.reshape(1, 32),
        jnp.pad(conv1_weight, ((0, 7), (0, 0))), conv2_weight, proj_weight, qkv_weight, out_weight,
        *spectrum_tables(), *filter_tables(), patch_table(),
    )
    vmem, anywhere = pl.BlockSpec(memory_space=pltpu.VMEM), pl.BlockSpec(memory_space=pl.ANY)
    dma = pltpu.SemaphoreType.DMA
    shape = jax.ShapeDtypeStruct((32, 8, D), BF)
    regrouped, attended = pl.pallas_call(
        whole_kernel,
        out_shape=(shape, shape),
        in_specs=[
            anywhere, vmem, vmem, vmem, vmem, anywhere, anywhere, anywhere, vmem,
            anywhere, anywhere, anywhere, anywhere, anywhere,
        ],
        out_specs=(vmem, vmem),
        scratch_shapes=[
            pltpu.VMEM((ROWS, EXT), F32),
            pltpu.VMEM((4, 288, N_FFT), BF),
            pltpu.VMEM((4, 288, N_FFT), BF),
            pltpu.VMEM((4, 288, 128), BF),
            pltpu.VMEM((544, 640), BF),
            pltpu.VMEM((8, 128, CH), BF),
            pltpu.VMEM((544, 41 * CH), BF),
            pltpu.VMEM((256, 20 * CH), BF),
            pltpu.VMEM((9 * CH, CH), BF),
            pltpu.VMEM((N_FFT, N_FFT), BF),
            pltpu.VMEM((N_FFT, N_FFT), BF),
            pltpu.VMEM((N_FFT // 2, 128), BF),
            pltpu.VMEM((N_FFT // 2, 128), BF),
            pltpu.VMEM((384, 640), BF),
            pltpu.VMEM((32, 160, D), BF),
            pltpu.VMEM((32, 32, WIDE), BF),
            pltpu.VMEM((32, 8, D), BF),
            pltpu.VMEM((4, 32, 8, D), BF),
            pltpu.VMEM((1024, 3 * PART), BF),
            pltpu.VMEM((4, 256, PART), BF),
            pltpu.VMEM((4, 256, PART), BF),
            dma((12,)), dma((2,)),
            dma((36,)), dma((36,)), dma((36,)), dma((36,)),
            dma((32,)), dma((32,)), dma((12,)), dma((12,)), dma((4,)), dma((4,)),
        ],
        compiler_params=pltpu.CompilerParams(
            vmem_limit_bytes=VMEM_LIMIT, collective_id=0, has_side_effects=True
        ),
        name="whole",
    )(*args)
    return regrouped.reshape(1, 32, 1, 8, D), attended.reshape(1, 32, 1, 8, D)


def solution(mesh):
    in_specs = (
        P(None, ("dp", "seq")), P(), P(), P(), P(), P(), P("dp", None), P("dp", None), P(None, "dp"),
    )
    out_specs = (P("dp", None, "seq", None, None), P("dp", None, "seq", None, None))
    return jax.shard_map(
        on_device, mesh=mesh, in_specs=in_specs, out_specs=out_specs, check_vma=False
    )
```

time: 237 us -> 98.4 us (0.42)
  waiting for transfers between devices: 131 us -> 0 us
  Pallas kernels: 32.6 us -> 91.8 us
  blocking collectives: 22.2 us -> 0 us
  between operations: 15.2 us -> 0.65 us
  matrix products: 12.8 us -> 0 us
  other arithmetic: 8.66 us -> 0 us
  starting transfers between devices: 4.69 us -> 0 us
  local copies, waits for them, and re-layouts: 9.18 us -> 5.7 us
    all_gather x4 -> x0, waiting for transfers between devices: 127 us -> none  [the longest x1 52.3 us: on_device(): proj = lax.all_gather(proj_weight, 'dp', axis=0, tiled=True)]
    pallas_call x1, Pallas kernels: 32.6 us -> 91.8 us  [on_device(): pl.pallas_call(whole_kernel, out_shape=(shape, shape), in_specs=[anywhere...]
    all_to_all x1 -> x0, blocking collectives: 22.2 us -> none  [on_device(): lax.all_to_all(ordered, 'dp', split_axis=0, concat_axis=0, tiled=True)]
    dot_general x4 -> x0, matrix products: 12.8 us -> none  [the longest x1 4.67 us: on_device(): mixed = jnp.dot(normed, weights_mix, preferred_element_type=F32).astype(BF)]
    slice x3 -> x0, local copies, waits for them, and re-layouts: 4.69 us -> none  [the longest x1 2.69 us: on_device(): key_piece[:, :, :D].reshape(number * local_count, HEADS, HEAD_DIM)]
    sub x1 -> x0, other arithmetic: 4.62 us -> none  [on_device(): masked - peak[:, :, None]]
    ppermute x1 -> x0, starting transfers between devices: 4.35 us -> none  [passed_along(): return lax.ppermute(block, axis, route)]
    unnamed x10 -> x5, local copies, waits for them, and re-layouts: 1.26 us -> 4.4 us
  transfers between devices with their start and end apart: 5 -> 0, of which waited for: 5 -> 0; matrix products, arithmetic and copies ran while one was open for 9% -> 0% of each run, Pallas kernels for 14% -> 0%
where the time goes in v1:
time: 98.4 us; the launch traced here: 98.2 us
  Pallas kernels  91.8 us (93%)
  local copies, waits for them, and re-layouts  5.7 us (6%)
    pallas_call x1, Pallas kernels, on_device(): pl.pallas_call(whole_kernel, out_shape=(shape, shape), in_specs=[anywhere...  91.8 us
    unnamed x5, local copies, waits for them, and re-layouts  4.4 us

profile of v1, /device:TPU:1, one launch (start us, length us, event | category | flops | bytes accessed | tf_op | source)
XLA Modules:
  0.0 98.2 jit_solution(6518431759615158915)
XLA Ops:
  0.6 1.3 %pad.4.conv1_in = bf16[16,256]{1,0:T(8,128)(2,1)} pad(bf16[9,256]{1,0:T(8,128)(2,1)} %param.18, bf16[]{:T(256)} %constant.12.clone.1), padding=0_7x0_0 | pad | bytes 12802 | tf_op jit(solution)/shard_map/jit(_pad)/pad | solution.py:594
  1.9 1.7 %copy.16.out_in = bf16[1024,32]{1,0:T(8,128)(2,1)} copy(bf16[1024,32]{0,1:T(8,128)(2,1)} %param.22) | data formatting | bytes 131072 | tf_op args[8]
  3.6 91.8 %whole.1 = (bf16[32,8,1024]{2,1,0:T(8,128)(2,1)}, bf16[32,8,1024]{2,1,0:T(8,128)(2,1)}) custom-call(f32[32,5120]{1,0:T(8,128)} %audio_in.1, s32[1,32]{1,0:T(1,128)} %bitcast.11, s32[1,32]{1,0:T(1,128)} %bitcast.12, s32[1,32]{1,0:T(1,128)} %bitcast.13, bf16[16,256]{1,0:T(8,128)(2,1)} %pad.4.conv1_in, bf16[2304,256]{1,0:T(8,128)(2,1)} %conv2_in.1, ...), custom_call_target="tpu_custom_call" | custom-call | tf_op jit(solution)/shard_map/whole/pallas_call | solution.py:600
  95.5 0.0 copy-start
  95.5 1.9 %copy.21 = bf16[1,32,1,8,1024]{4,3,2,1,0:T(8,128)(2,1)} copy(bf16[1,32,1,8,1024]{4,3,2,1,0:T(8,128)(2,1)} %bitcast.10) | data formatting | bytes 1048576
  97.4 0.0 copy-done
  97.4 0.8 copy.22
Async XLA Ops:
  95.5 1.9 %copy-start = (bf16[32,8,1024]{2,1,0:T(8,128)(2,1)S(1)}, bf16[32,8,1024]{2,1,0:T(8,128)(2,1)}, u32[]{:S(2)}) copy-start(bf16[32,8,1024]{2,1,0:T(8,128)(2,1)} %get-tuple-element.5) | copy-start | bytes 1572868

commit v2 on v1

--- a/solution.py
+++ b/solution.py
@@ -101,34 +101,41 @@
         frames_low[q, rows, :] = low
 
 
-def mel_step(q, frames_high, frames_low, dft_high, dft_low, mel_high, mel_low, log_mel):
-    high, low = frames_high[q], frames_low[q]
+def mel_of(high, low, dft_high, dft_low, mel_high, mel_low):
     spectrum = mm(high, dft_high[...]) + mm(high, dft_low[...]) + mm(low, dft_high[...])
     half = N_FFT // 2
     power = spectrum[:, :half] * spectrum[:, :half] + spectrum[:, half:] * spectrum[:, half:]
     high, low = halves(power)
     mel = mm(high, mel_high[...]) + mm(high, mel_low[...]) + mm(low, mel_high[...])
-    log_mel[q] = jnp.log(mel + EPS_LOG).astype(BF)
-
-
-def make_patches(log_mel, patch_map, patches):
-    even = jnp.concatenate([log_mel[0], log_mel[1], log_mel[2]], axis=1)
-    patches[:288, :] = mm(even, patch_map[...]).astype(BF)
-    odd = jnp.concatenate([log_mel[2, :256], log_mel[3, :256], log_mel[0, 32:]], axis=1)
-    patches[288:, :] = mm(odd, patch_map[...]).astype(BF)
+    return jnp.log(mel + EPS_LOG).astype(BF)
+
+
+def late_patches(log_mel, patch_map, patches):
+    even = jnp.concatenate([log_mel[0, 64:], log_mel[1, 64:], log_mel[2, 64:]], axis=1)
+    patches[:224, :] = mm(even, patch_map[...]).astype(BF)
+    odd = jnp.concatenate([log_mel[2, 64:256], log_mel[3, 64:256], log_mel[0, 96:]], axis=1)
+    patches[224:416, :] = mm(odd, patch_map[...]).astype(BF)
+
+
+def early_patches(log_mel, patch_map, patches):
+    even = jnp.concatenate([log_mel[0, :64], log_mel[1, :64], log_mel[2, :64]], axis=1)
+    odd = jnp.concatenate([log_mel[2, :64], log_mel[3, :64], log_mel[0, 32:96]], axis=1)
+    patches[416:, :] = mm(jnp.concatenate([even, odd], axis=0), patch_map[...]).astype(BF)
 
 
 def spread_taps(conv1, taps):
     taps[...] = jnp.zeros_like(taps)
     for j in range(8):
-        taps[j, 16 * j : 16 * j + 16, :] = conv1[...]
-
-
-def conv1_step(g, patches, taps, first):
-    block, j = g // 8, g % 8
-    lanes = pl.ds(pl.multiple_of(block * 128, 128), 128)
-    result = mm(patches[:, lanes], taps[j])
-    first[:, pl.ds(pl.multiple_of(g * CH + CH, CH), CH)] = jnp.maximum(result, 0.0).astype(BF)
+        taps[j, 16 * j : 16 * j + 9, :] = conv1[...]
+
+
+def conv1_step(block, j, late, patches, taps, first):
+    lanes = slice(block * 128, block * 128 + 128)
+    target = pl.ds(pl.multiple_of((block * 8 + j + 1) * CH, CH), CH)
+    rows, count = (slice(0, 416), 224) if late else (slice(416, 544), 64)
+    result = jnp.maximum(mm(patches[rows, lanes], taps[j]), 0.0).astype(BF)
+    first[slice(64, 288) if late else slice(0, 64), target] = result[:count]
+    first[slice(352, 544) if late else slice(288, 352), target] = result[count:]
 
 
 def conv2_step(h, first, conv2, features):
@@ -293,7 +300,7 @@
             )
         )
     ]
-    parts = [
+    parts = [local(out_in, wide.at[me, :, pl.ds(3 * PART, D)], 12)] + [
         local(
             qkv_in.at[:, pl.ds(pl.multiple_of(third * D + z * PART, 128), PART)],
             wide.at[me, :, pl.ds(third * PART, PART)],
@@ -321,12 +328,7 @@
     spread_taps(conv1_in, taps)
     first[:, :CH] = jnp.zeros((544, CH), BF)
     ext[:, RIM + SPAN :] = jnp.zeros((ROWS, EXT - RIM - SPAN), F32)
-    turn = jnp.where(
-        lax.broadcasted_iota(jnp.int32, (32, 32), 0) == lax.broadcasted_iota(jnp.int32, (32, 32), 1), 1.0, 0.0
-    ).astype(BF)
-    wide[me, :, 3 * PART :] = nt(turn, out_in[...]).astype(BF)
     pl.semaphore_wait(barrier, 36)
-
     halo = pltpu.make_async_remote_copy(
         src_ref=audio_in.at[:, pl.ds(SPAN - RIM, RIM)],
         dst_ref=ext.at[:, pl.ds(0, RIM)],
@@ -340,60 +342,69 @@
     ring.begin()
 
     loads[0].wait()
+
+    @pl.loop(2, 9)
+    def _(p):
+        frame_step(p, ext, frames_high, frames_low)
+
+    for load in loads[1:5]:
+        load.wait()
+    tables = (dft_high, dft_low, mel_high, mel_low)
+
+    for q in range(4):
+        log_mel[q, 64:, :] = mel_of(frames_high[q, 64:, :], frames_low[q, 64:, :], *tables)
+
+    loads[5].wait()
+    late_patches(log_mel, patch_map, patches)
+
+    def conv1_run(late):
+        @pl.loop(0, 8)
+        def _(j):
+            for block in range(5):
+                conv1_step(block, j, late, patches, taps, first)
+
+    def conv2_run(low, high):
+        @pl.loop(low, high)
+        def _(group):
+            for i in range(4):
+                conv2_step(group * 4 + i, first, conv2, features)
+
+    conv1_run(True)
+    ring.pass_a()
+    ring.pass_b(0)
     halo.wait_recv()
 
     @pl.when(line == 0)
     def _():
         ext[:, :RIM] = jnp.zeros((ROWS, RIM), F32)
 
-    @pl.loop(0, 9)
+    @pl.loop(0, 2)
     def _(p):
         frame_step(p, ext, frames_high, frames_low)
 
-    for load in loads[1:5]:
-        load.wait()
-
-    @pl.loop(0, 4)
-    def _(q):
-        mel_step(q, frames_high, frames_low, dft_high, dft_low, mel_high, mel_low, log_mel)
-
-    loads[5].wait()
-    make_patches(log_mel, patch_map, patches)
-
-    def conv1_run(low, high):
-        @pl.loop(low, high)
-        def _(g):
-            conv1_step(g, patches, taps, first)
-
-    def conv2_run(low, high):
-        @pl.loop(low, high)
-        def _(h):
-            conv2_step(h, first, conv2, features)
-
-    conv1_run(0, 8)
-    ring.pass_a()
-    conv1_run(8, 16)
-    ring.pass_b(0)
-    conv1_run(16, 32)
+    early = mel_of(
+        frames_high[:, :64, :].reshape(256, N_FFT), frames_low[:, :64, :].reshape(256, N_FFT), *tables
+    )
+    for q in range(4):
+        log_mel[q, :64, :] = early[64 * q : 64 * q + 64]
+    early_patches(log_mel, patch_map, patches)
+    conv1_run(False)
     ring.end_a()
-    conv1_run(32, 40)
     loads[6].wait()
-    conv2_run(0, 4)
+    conv2_run(0, 2)
     ring.pass_b(-1)
-    conv2_run(4, 8)
+    ring.pass_b(1)
     ring.end_b(0)
-    ring.pass_b(1)
-    conv2_run(8, 12)
-    conv2_run(12, 16)
+    conv2_run(2, 4)
     ring.pass_b(2)
+    conv2_run(4, 5)
     ring.end_b(-1)
-    conv2_run(16, 20)
     ring.end_b(1)
     ring.end_b(2)
-    ring.from_sibling()
-    loads[7].wait()
-
-    projected = mm(features[...], proj[...].reshape(20 * CH, D)).astype(BF)
+    for part in parts:
+        part.wait()
+    wide_ring = Ring(wide.at[me], wide, wide_send, wide_recv, place)
+    wide_ring.begin()
     tile_map = jnp.where(
         lax.broadcasted_iota(jnp.int32, (32, 256), 1) % 32 == lax.broadcasted_iota(jnp.int32, (32, 256), 0),
         1.0, 0.0,
@@ -403,10 +414,14 @@
     out_index = lax.broadcasted_iota(jnp.int32, (256, 256), 0)
     in_index = lax.broadcasted_iota(jnp.int32, (256, 256), 1)
     routing = jnp.where((slots_wide == out_index // 8) & (in_index // 32 == out_index % 8), 1.0, 0.0).astype(BF)
+    ring.from_sibling()
+    loads[7].wait()
+
+    projected = mm(features[...], proj[...].reshape(20 * CH, D)).astype(BF)
     rows_out[...] = mm(routing, projected).reshape(32, 8, D).astype(BF)
 
     def row_copy(offset):
-        target = lax.rem(me + offset, 32)
+        target = lax.rem(x + 4 - offset // 8, 4) * 8 + lax.rem(me + offset, 8)
         return pltpu.make_async_remote_copy(
             src_ref=rows_out.at[target],
             dst_ref=rows_all.at[z, me],
@@ -421,10 +436,8 @@
         row_copy(offset).start()
 
     mine = local(rows_out.at[me], rows_all.at[z, me], 11)
-    for part in parts:
-        part.wait()
-    wide_ring = Ring(wide.at[me], wide, wide_send, wide_recv, place)
-    wide_ring.begin()
+    wide_ring.pass_a()
+    wide_ring.pass_b(0)
     mine.wait()
 
     def z_copy(origin, chunk, upwards, index):
@@ -475,17 +488,15 @@
         copy.start()
         z_copies.append(copy)
 
-    wide_ring.pass_a()
+    wide_ring.end_a()
     z_forward(0)
-    wide_ring.pass_b(0)
-    wide_ring.end_a()
-    z_forward(1)
     wide_ring.end_b(0)
     wide_ring.pass_b(-1)
     wide_ring.pass_b(1)
-    z_forward(2)
+    z_forward(1)
     wide_ring.pass_b(2)
     wide_ring.end_b(-1)
+    z_forward(2)
     wide_ring.end_b(1)
     wide_ring.end_b(2)
     z_forward(3)
@@ -515,11 +526,14 @@
         return (sample >= begin) & (sample < begin + span)
 
     key_index = lax.broadcasted_iota(jnp.int32, (1, 1024), 1)
-    key_valid = valid_of(key_index // 256, key_index % 256)
-    scale = HEAD_DIM ** (-0.5)
+    bias = jnp.where(valid_of(key_index // 256, key_index % 256), 0.0, MASKED)
+    scale = HEAD_DIM ** (-0.5) * math.log2(math.e)
+
+    def context_target(step):
+        return lax.rem(z + 2 + step - step // 2 * (2 * step - 1), 4)
 
     def context_copy(step):
-        target = lax.rem(z + 3 - step, 4)
+        target = context_target(step)
         return pltpu.make_async_remote_copy(
             src_ref=context_out.at[target],
             dst_ref=context_in.at[z],
@@ -531,17 +545,15 @@
 
     @pl.loop(0, 4)
     def _(step):
-        target = lax.rem(z + 3 - step, 4)
+        target = context_target(step)
         rows = pl.ds(pl.multiple_of(target * 256, 256), 256)
         for head in range(2):
             lanes = slice(head * HEAD_DIM, (head + 1) * HEAD_DIM)
             query = mixed[rows, lanes]
             key = mixed[:, PART + head * HEAD_DIM : PART + (head + 1) * HEAD_DIM]
             value = mixed[:, 2 * PART + head * HEAD_DIM : 2 * PART + (head + 1) * HEAD_DIM]
-            masked = jnp.where(key_valid, nt(query, key) * scale, MASKED)
-            weights = jnp.where(
-                key_valid, jnp.exp(masked - jnp.max(masked, axis=1, keepdims=True)), 0.0
-            )
+            scores = nt(query, key) * scale + bias
+            weights = jnp.exp2(scores - jnp.max(scores, axis=1, keepdims=True))
             total = jnp.sum(weights, axis=1, keepdims=True)
             context_out[target, :, lanes] = (mm(weights.astype(BF), value) / total).astype(BF)
 
@@ -591,7 +603,7 @@
 ):
     args = (
         audio, starts.reshape(1, 32), lengths.reshape(1, 32), slots.reshape(1, 32),
-        jnp.pad(conv1_weight, ((0, 7), (0, 0))), conv2_weight, proj_weight, qkv_weight, out_weight,
+        conv1_weight, conv2_weight, proj_weight, qkv_weight, out_weight.T,
         *spectrum_tables(), *filter_tables(), patch_table(),
     )
     vmem, anywhere = pl.BlockSpec(memory_space=pltpu.VMEM), pl.BlockSpec(memory_space=pl.ANY)
@@ -601,7 +613,7 @@
         whole_kernel,
         out_shape=(shape, shape),
         in_specs=[
-            anywhere, vmem, vmem, vmem, vmem, anywhere, anywhere, anywhere, vmem,
+            anywhere, vmem, vmem, vmem, vmem, anywhere, anywhere, anywhere, anywhere,
             anywhere, anywhere, anywhere, anywhere, anywhere,
         ],
         out_specs=(vmem, vmem),
@@ -627,7 +639,7 @@
             pltpu.VMEM((1024, 3 * PART), BF),
             pltpu.VMEM((4, 256, PART), BF),
             pltpu.VMEM((4, 256, PART), BF),
-            dma((12,)), dma((2,)),
+            dma((13,)), dma((2,)),
             dma((36,)), dma((36,)), dma((36,)), dma((36,)),
             dma((32,)), dma((32,)), dma((12,)), dma((12,)), dma((4,)), dma((4,)),
         ],

time: 98.4 us -> 88.5 us (0.90)
  Pallas kernels: 91.8 us -> 85 us
  local copies, waits for them, and re-layouts: 5.7 us -> 2.72 us
    pallas_call x1, Pallas kernels: 91.8 us -> 85 us  [on_device(): pl.pallas_call(whole_kernel, out_shape=(shape, shape), in_specs=[anywhere...]
    unnamed x5 -> x4, local copies, waits for them, and re-layouts: 4.4 us -> 2.72 us
    pad x1 -> x0, local copies, waits for them, and re-layouts: 1.3 us -> none  [on_device(): jnp.pad(conv1_weight, ((0, 7), (0, 0)))]
where the time goes in v2:
time: 88.5 us; the launch traced here: 88.4 us
  Pallas kernels  85 us (96%)
  local copies, waits for them, and re-layouts  2.72 us (3%)
    pallas_call x1, Pallas kernels, on_device(): pl.pallas_call(whole_kernel, out_shape=(shape, shape), in_specs=[anywhere...  85 us
    unnamed x4, local copies, waits for them, and re-layouts  2.72 us

profile of v2, /device:TPU:1, one launch (start us, length us, event | category | flops | bytes accessed | tf_op | source)
XLA Modules:
  0.0 88.4 jit_solution(7884420752525482700)
XLA Ops:
  0.6 85.0 %whole.1 = (bf16[32,8,1024]{2,1,0:T(8,128)(2,1)}, bf16[32,8,1024]{2,1,0:T(8,128)(2,1)}) custom-call(f32[32,5120]{1,0:T(8,128)} %audio_in.1, s32[1,32]{1,0:T(1,128)} %bitcast.13, s32[1,32]{1,0:T(1,128)} %bitcast.14, s32[1,32]{1,0:T(1,128)} %bitcast.15, bf16[9,256]{1,0:T(8,128)(2,1)} %conv1_in.1, bf16[2304,256]{1,0:T(8,128)(2,1)} %conv2_in.1, ...), custom_call_target="tpu_custom_call" | custom-call | tf_op jit(solution)/shard_map/whole/pallas_call | solution.py:612
  85.6 0.0 copy-start
  85.6 1.9 %copy.20 = bf16[1,32,1,8,1024]{4,3,2,1,0:T(8,128)(2,1)} copy(bf16[1,32,1,8,1024]{4,3,2,1,0:T(8,128)(2,1)} %bitcast.11) | data formatting | bytes 1048576
  87.6 0.0 copy-done
  87.6 0.8 copy.21
Async XLA Ops:
  85.6 1.9 %copy-start = (bf16[32,8,1024]{2,1,0:T(8,128)(2,1)S(1)}, bf16[32,8,1024]{2,1,0:T(8,128)(2,1)}, u32[]{:S(2)}) copy-start(bf16[32,8,1024]{2,1,0:T(8,128)(2,1)} %get-tuple-element.5) | copy-start | bytes 1572868

commit v3 on v2

--- a/solution.py
+++ b/solution.py
@@ -156,7 +156,8 @@
 
 MESH_ID = pl.DeviceIdType.MESH
 PART = 2 * HEAD_DIM
-WIDE = 3 * PART + D
+PAIR = 2 * PART
+WIDE = 3 * PAIR + D
 
 
 class Ring:
@@ -266,9 +267,9 @@
     regrouped, attended,
     ext, frames_high, frames_low, log_mel, patches, taps, first, features,
     conv2, dft_high, dft_low, mel_high, mel_low, patch_map,
-    proj, wide, rows_out, rows_all, mixed, context_out, context_in,
+    proj, wide, rows_out, rows_own, rows_all, mixed, context_out, context_in,
     local_sem, halo_sem, proj_send, proj_recv, wide_send, wide_recv,
-    row_send, row_recv, z_send, z_recv, context_send, context_recv,
+    row_send, row_recv, z_send, z_recv, pass_send, pass_recv, keep_sem, context_send, context_recv,
 ):
     me, z = lax.axis_index("dp"), lax.axis_index("seq")
     x, y, core = me // 8, me // 2 % 4, me % 2
@@ -278,7 +279,12 @@
     place = (core, a, b, sa, sb, sibling)
     line = me * 4 + z
     after, before = lax.rem(line + 1, 128), lax.rem(line + 127, 128)
-    up, down = lax.rem(z + 1, 4), lax.rem(z + 3, 4)
+    keeper = core == z // 2
+    helper = core != z // 2
+    row = me - core + z // 2
+    partner, cross = z + 1 - 2 * (z % 2), 3 - z
+    beyond = 3 - partner
+    pair = z % 2 * 2 + core
 
     def local(source, target, index):
         copy = pltpu.make_async_copy(source, target, local_sem.at[index])
@@ -300,10 +306,10 @@
             )
         )
     ]
-    parts = [local(out_in, wide.at[me, :, pl.ds(3 * PART, D)], 12)] + [
+    parts = [local(out_in, wide.at[me, :, pl.ds(3 * PAIR, D)], 12)] + [
         local(
-            qkv_in.at[:, pl.ds(pl.multiple_of(third * D + z * PART, 128), PART)],
-            wide.at[me, :, pl.ds(third * PART, PART)],
+            qkv_in.at[:, pl.ds(pl.multiple_of(third * D + z % 2 * PAIR, 128), PAIR)],
+            wide.at[me, :, pl.ds(third * PAIR, PAIR)],
             8 + third,
         )
         for third in range(3)
@@ -321,6 +327,13 @@
         pl.semaphore_signal(
             barrier, inc=1, device_id={"seq": lax.rem(z + offset, 4)}, device_id_type=MESH_ID
         )
+    for offset in range(1, 4):
+        pl.semaphore_signal(
+            barrier,
+            inc=1,
+            device_id={"dp": sibling, "seq": lax.rem(z + offset, 4)},
+            device_id_type=MESH_ID,
+        )
     for other in (after, before):
         pl.semaphore_signal(
             barrier, inc=1, device_id={"dp": other // 4, "seq": other % 4}, device_id_type=MESH_ID
@@ -328,7 +341,7 @@
     spread_taps(conv1_in, taps)
     first[:, :CH] = jnp.zeros((544, CH), BF)
     ext[:, RIM + SPAN :] = jnp.zeros((ROWS, EXT - RIM - SPAN), F32)
-    pl.semaphore_wait(barrier, 36)
+    pl.semaphore_wait(barrier, 39)
     halo = pltpu.make_async_remote_copy(
         src_ref=audio_in.at[:, pl.ds(SPAN - RIM, RIM)],
         dst_ref=ext.at[:, pl.ds(0, RIM)],
@@ -424,7 +437,7 @@
         target = lax.rem(x + 4 - offset // 8, 4) * 8 + lax.rem(me + offset, 8)
         return pltpu.make_async_remote_copy(
             src_ref=rows_out.at[target],
-            dst_ref=rows_all.at[z, me],
+            dst_ref=rows_own.at[me],
             send_sem=row_send.at[offset],
             recv_sem=row_recv.at[me],
             device_id={"dp": target},
@@ -435,24 +448,57 @@
     def _(offset):
         row_copy(offset).start()
 
-    mine = local(rows_out.at[me], rows_all.at[z, me], 11)
+    mine = local(rows_out.at[me], rows_own.at[me], 11)
     wide_ring.pass_a()
     wide_ring.pass_b(0)
     mine.wait()
 
-    def z_copy(origin, chunk, upwards, index):
-        block = rows_all.at[origin, pl.ds(pl.multiple_of(chunk * 8, 8), 8)]
+    chunks = [lax.rem(x + index, 4) for index in range(4)]
+    origins = (z, partner, cross, beyond)
+
+    def part_of(buffer, index):
+        return buffer.at[pl.ds(pl.multiple_of(chunks[index] * 8, 8), 8)]
+
+    def row_part(origin, index):
+        return rows_all.at[origin, pl.ds(pl.multiple_of(chunks[index] * 8, 8), 8)]
+
+    def to_plane(source, origin, index, base, plane):
         return pltpu.make_async_remote_copy(
-            src_ref=block,
-            dst_ref=block,
-            send_sem=z_send.at[index],
-            recv_sem=z_recv.at[index],
-            device_id={"seq": up if upwards else down},
+            src_ref=source,
+            dst_ref=row_part(origin, index),
+            send_sem=z_send.at[base + index],
+            recv_sem=z_recv.at[base + index],
+            device_id={"seq": plane},
             device_id_type=MESH_ID,
         )
 
-    z_copies = []
-    chunks = [lax.rem(x + index, 4) for index in range(4)]
+    def to_sibling(source, place, index):
+        return pltpu.make_async_remote_copy(
+            src_ref=source,
+            dst_ref=row_part(origins[place], index),
+            send_sem=pass_send.at[4 * place + index],
+            recv_sem=pass_recv.at[4 * place + index],
+            device_id={"dp": sibling},
+            device_id_type=MESH_ID,
+        )
+
+    def arrived(place, index, base):
+        block = row_part(origins[place], index)
+        to_plane(block, origins[place], index, base, partner).wait_recv()
+        return block
+
+    def own_to_partner(index):
+        return to_plane(part_of(rows_own, index), z, index, 0, partner)
+
+    def own_across(index):
+        return to_plane(part_of(rows_own, index), z, index, 4, cross)
+
+    def cross_to_partner(index):
+        return to_plane(row_part(cross, index), cross, index, 8, partner)
+
+    def own_copy(index):
+        return pltpu.make_async_copy(part_of(rows_own, index), row_part(z, index), keep_sem.at[index])
+
     for index in range(4):
         @pl.loop(0, 8)
         def _(step):
@@ -460,7 +506,7 @@
 
             @pl.when(source != me)
             def _():
-                block = rows_all.at[z, source]
+                block = rows_own.at[source]
                 pltpu.make_async_remote_copy(
                     src_ref=block,
                     dst_ref=block,
@@ -470,63 +516,97 @@
                     device_id_type=MESH_ID,
                 ).wait_recv()
 
-        for direction in range(2):
-            copy = z_copy(z, chunks[index], direction == 0, 6 * direction + index)
-            copy.start()
-            z_copies.append(copy)
-
-    def z_wait(origin, chunk, index):
-        z_copy(origin, chunk, True, index).wait_recv()
-
-    def z_forward(index):
-        z_wait(down, chunks[index], index)
-        z_wait(up, chunks[index], 6 + index)
-        if index < 2:
-            copy = z_copy(down, chunks[index], True, 4 + index)
-        else:
-            copy = z_copy(up, chunks[index], False, 6 + 2 + index)
-        copy.start()
-        z_copies.append(copy)
-
+        @pl.when(keeper)
+        def _():
+            own_to_partner(index).start()
+            to_sibling(part_of(rows_own, index), 0, index).start()
+            own_copy(index).start()
+
+        @pl.when(helper)
+        def _():
+            own_across(index).start()
+
+    def pass_cross(index):
+        @pl.when(keeper)
+        def _():
+            block = arrived(2, index, 4)
+            cross_to_partner(index).start()
+            to_sibling(block, 2, index).start()
+
+    def pass_partner(index):
+        @pl.when(keeper)
+        def _():
+            to_sibling(arrived(1, index, 0), 1, index).start()
+
+    def pass_beyond(index):
+        @pl.when(keeper)
+        def _():
+            to_sibling(arrived(3, index, 8), 3, index).start()
+
+    pass_cross(0)
     wide_ring.end_a()
-    z_forward(0)
+    pass_cross(1)
+    pass_partner(0)
     wide_ring.end_b(0)
+    pass_cross(2)
+    pass_partner(1)
     wide_ring.pass_b(-1)
+    pass_cross(3)
+    pass_partner(2)
     wide_ring.pass_b(1)
-    z_forward(1)
+    pass_partner(3)
     wide_ring.pass_b(2)
+    pass_beyond(0)
     wide_ring.end_b(-1)
-    z_forward(2)
     wide_ring.end_b(1)
+    pass_beyond(1)
     wide_ring.end_b(2)
-    z_forward(3)
     wide_ring.from_sibling()
+
+    @pl.when(keeper)
+    def _():
+        for index in range(4):
+            own_copy(index).wait()
+
+    def helped(place):
+        @pl.when(helper)
+        def _():
+            for index in range(4):
+                to_sibling(row_part(origins[place], index), place, index).wait_recv()
 
     def mix(origin):
         values = rows_all[origin].astype(F32).reshape(256, D)
-        result = mm(normalised(values), wide[:, :, : 3 * PART].reshape(D, 3 * PART))
-        mixed[pl.ds(pl.multiple_of(origin * 256, 256), 256), :] = result.astype(BF)
-
+        normed = normalised(values)
+        rows = pl.ds(pl.multiple_of(origin * 256, 256), 256)
+        for third in range(3):
+            lanes = pl.ds(pl.multiple_of(third * PAIR + core * PART, 128), PART)
+            result = mm(normed, wide[:, :, lanes].reshape(D, PART))
+            mixed[rows, third * PART : third * PART + PART] = result.astype(BF)
+
+    helped(0)
     mix(z)
-    mix(down)
-    mix(up)
-    opposite = lax.rem(z + 2, 4)
-    for index in range(2):
-        z_wait(opposite, chunks[index], 4 + index)
-        z_wait(opposite, chunks[2 + index], 6 + 4 + index)
-    mix(opposite)
-
-    chosen = slots[...] == me
-    begin = jnp.sum(jnp.where(chosen, starts[...].astype(F32), 0.0), axis=1, keepdims=True)
-    span = jnp.sum(jnp.where(chosen, lengths[...].astype(F32), 0.0), axis=1, keepdims=True)
-
-    def valid_of(owner, index):
+    pass_beyond(2)
+    helped(1)
+    mix(partner)
+    helped(2)
+    mix(cross)
+    pass_beyond(3)
+    helped(3)
+    mix(beyond)
+
+    def bounds(owner):
+        chosen = slots[...] == owner
+        begin = jnp.sum(jnp.where(chosen, starts[...].astype(F32), 0.0), axis=1, keepdims=True)
+        span = jnp.sum(jnp.where(chosen, lengths[...].astype(F32), 0.0), axis=1, keepdims=True)
+        return begin, begin + span
+
+    def valid_of(owner, index, limits):
         frame = (index // 8 * 4 + owner) * 8 + index % 8
         sample = (frame * (4 * HOP)).astype(F32)
-        return (sample >= begin) & (sample < begin + span)
+        return (sample >= limits[0]) & (sample < limits[1])
 
     key_index = lax.broadcasted_iota(jnp.int32, (1, 1024), 1)
-    bias = jnp.where(valid_of(key_index // 256, key_index % 256), 0.0, MASKED)
+    bias = jnp.where(valid_of(key_index // 256, key_index % 256, bounds(row)), 0.0, MASKED)
     scale = HEAD_DIM ** (-0.5) * math.log2(math.e)
 
     def context_target(step):
@@ -536,10 +616,10 @@
         target = context_target(step)
         return pltpu.make_async_remote_copy(
             src_ref=context_out.at[target],
-            dst_ref=context_in.at[z],
+            dst_ref=context_in.at[pair],
             send_sem=context_send.at[step],
-            recv_sem=context_recv.at[z],
-            device_id={"seq": target},
+            recv_sem=context_recv.at[pair],
+            device_id={"dp": row, "seq": target},
             device_id_type=MESH_ID,
         )
 
@@ -561,25 +641,38 @@
         def _():
             context_copy(step).start()
 
-    context_in[z] = context_out[z]
-    for offset in range(1, 4):
-        other = lax.rem(z + offset, 4)
+    @pl.when(keeper)
+    def _():
+        context_in[pair] = context_out[z]
+
+    @pl.when(helper)
+    def _():
+        context_copy(3).start()
+
+    def context_wait(other):
         pltpu.make_async_remote_copy(
             src_ref=context_in.at[other],
             dst_ref=context_in.at[other],
             send_sem=context_send.at[3],
             recv_sem=context_recv.at[other],
-            device_id={"seq": up},
+            device_id={"dp": row, "seq": cross},
             device_id_type=MESH_ID,
         ).wait_recv()
 
+    for offset in range(1, 4):
+        context_wait(lax.rem(pair + offset, 4))
+
+    @pl.when(helper)
+    def _():
+        context_wait(pair)
+
     output = jnp.zeros((256, D), F32)
     for part in range(4):
-        start = 3 * PART + part * PART
+        start = 3 * PAIR + part * PART
         output += nt(context_in[part], wide[:, :, start : start + PART].reshape(D, PART))
-    row_valid = valid_of(z, lax.broadcasted_iota(jnp.int32, (256, 1), 0))
+    row_valid = valid_of(z, lax.broadcasted_iota(jnp.int32, (256, 1), 0), bounds(me))
     attended[...] = jnp.where(row_valid, output, 0.0).reshape(32, 8, D).astype(BF)
-    own = rows_all[z].astype(F32).reshape(256, D)
+    own = rows_own[...].astype(F32).reshape(256, D)
     regrouped[...] = jnp.where(row_valid, own, 0.0).reshape(32, 8, D).astype(BF)
 
     halo.wait_send()
@@ -590,8 +683,19 @@
     def _(offset):
         row_copy(offset).wait_send()
 
-    for copy in z_copies:
-        copy.wait_send()
+    @pl.when(keeper)
+    def _():
+        for index in range(4):
+            own_to_partner(index).wait_send()
+            cross_to_partner(index).wait_send()
+            for place in range(4):
+                to_sibling(part_of(rows_own, index), place, index).wait_send()
+
+    @pl.when(helper)
+    def _():
+        for index in range(4):
+            own_across(index).wait_send()
+        context_copy(3).wait_send()
 
     @pl.loop(0, 3)
     def _(step):
@@ -635,13 +739,14 @@
             pltpu.VMEM((32, 160, D), BF),
             pltpu.VMEM((32, 32, WIDE), BF),
             pltpu.VMEM((32, 8, D), BF),
+            pltpu.VMEM((32, 8, D), BF),
             pltpu.VMEM((4, 32, 8, D), BF),
             pltpu.VMEM((1024, 3 * PART), BF),
             pltpu.VMEM((4, 256, PART), BF),
             pltpu.VMEM((4, 256, PART), BF),
             dma((13,)), dma((2,)),
             dma((36,)), dma((36,)), dma((36,)), dma((36,)),
-            dma((32,)), dma((32,)), dma((12,)), dma((12,)), dma((4,)), dma((4,)),
+            dma((32,)), dma((32,)), dma((12,)), dma((12,)), dma((16,)), dma((16,)), dma((4,)), dma((4,)), dma((4,)),
         ],
         compiler_params=pltpu.CompilerParams(
             vmem_limit_bytes=VMEM_LIMIT, collective_id=0, has_side_effects=True

time: 88.5 us -> 87.2 us (0.985)
  Pallas kernels: 85 us -> 83.7 us
    pallas_call x1, Pallas kernels: 85 us -> 83.7 us  [on_device(): pl.pallas_call(whole_kernel, out_shape=(shape, shape), in_specs=[anywhere...]
where the time goes in v3:
time: 87.2 us; the launch traced here: 87.1 us
  Pallas kernels  83.7 us (96%)
  local copies, waits for them, and re-layouts  2.72 us (3%)
    pallas_call x1, Pallas kernels, on_device(): pl.pallas_call(whole_kernel, out_shape=(shape, shape), in_specs=[anywhere...  83.7 us
    unnamed x4, local copies, waits for them, and re-layouts  2.72 us

profile of v3, /device:TPU:1, one launch (start us, length us, event | category | flops | bytes accessed | tf_op | source)
XLA Modules:
  0.0 87.1 jit_solution(248449316433999537)
XLA Ops:
  0.6 83.7 %whole.1 = (bf16[32,8,1024]{2,1,0:T(8,128)(2,1)}, bf16[32,8,1024]{2,1,0:T(8,128)(2,1)}) custom-call(f32[32,5120]{1,0:T(8,128)} %audio_in.1, s32[1,32]{1,0:T(1,128)} %bitcast.13, s32[1,32]{1,0:T(1,128)} %bitcast.14, s32[1,32]{1,0:T(1,128)} %bitcast.15, bf16[9,256]{1,0:T(8,128)(2,1)} %conv1_in.1, bf16[2304,256]{1,0:T(8,128)(2,1)} %conv2_in.1, ...), custom_call_target="tpu_custom_call" | custom-call | tf_op jit(solution)/shard_map/whole/pallas_call | solution.py:716
  84.3 0.0 copy-start
  84.3 1.9 %copy.20 = bf16[1,32,1,8,1024]{4,3,2,1,0:T(8,128)(2,1)} copy(bf16[1,32,1,8,1024]{4,3,2,1,0:T(8,128)(2,1)} %bitcast.11) | data formatting | bytes 1048576
  86.3 0.0 copy-done
  86.3 0.8 copy.21
Async XLA Ops:
  84.3 1.9 %copy-start = (bf16[32,8,1024]{2,1,0:T(8,128)(2,1)S(1)}, bf16[32,8,1024]{2,1,0:T(8,128)(2,1)}, u32[]{:S(2)}) copy-start(bf16[32,8,1024]{2,1,0:T(8,128)(2,1)} %get-tuple-element.5) | copy-start | bytes 1572868

commit v4 on v3

--- a/solution.py
+++ b/solution.py
@@ -28,7 +28,7 @@
 EPS_LOG = 1e-06
 EPS_NORM = 1e-05
 MASKED = -1e30
-VMEM_LIMIT = 62 * 1024 * 1024
+VMEM_LIMIT = 56 * 1024 * 1024
 
 
 def mel_table(size, bands):
@@ -177,9 +177,13 @@
         step = self.rows // 2
         return self.buffer.at[index, pl.ds(half * step, step)]
 
+    def origin(self, half):
+        step = self.rows // 2
+        return self.source if half is None else self.source.at[pl.ds(half * step, step)]
+
     def put(self, index, half, target, slot, own=False):
         copy = pltpu.make_async_remote_copy(
-            src_ref=self.source if own else self.part(index, half),
+            src_ref=self.origin(half) if own else self.part(index, half),
             dst_ref=self.part(index, half),
             send_sem=self.send.at[self.count],
             recv_sem=self.recv.at[slot],
@@ -200,25 +204,31 @@
             device_id_type=MESH_ID,
         ).wait_recv()
 
+    def to_both(self, index, above, below, base, line, own=False):
+        for target, half, slot in ((above, 0, 0), (below, 1, 1)):
+            self.put(index, half, target, base + slot, own)
+            self.put(index, 1 - half, target, 36 + 2 * line + slot, own)
+
+    def pass_both(self, lower, upper, above, below, base):
+        self.got(lower, 0, base)
+        self.put(lower, 0, above, base + 2)
+        self.got(upper, 1, base + 1)
+        self.put(upper, 1, below, base + 3)
+
     def to_b(self, da, own=False):
         index = self.shard(da, 0)
-        base = 4 + 4 * (da + 1)
-        self.put(index, None, self.shard(0, 1), base, own)
-        self.put(index, None, self.shard(0, -1), base + 1, own)
+        self.to_both(index, self.shard(0, 1), self.shard(0, -1), 4 + 4 * (da + 1), da + 2, own)
         self.put(index, None, self.sibling, 20 + 4 * (da + 1) + 1, own)
 
     def begin(self):
-        index = self.shard(0, 0)
-        self.put(index, None, self.shard(1, 0), 0, True)
-        self.put(index, None, self.shard(-1, 0), 1, True)
-        self.to_b(0, True)
+        self.to_both(self.shard(0, 0), self.shard(1, 0), self.shard(-1, 0), 0, 0, True)
 
     def pass_a(self):
-        for da, half, slot in ((-1, 0, 0), (1, 1, 1)):
-            index = self.shard(da, 0)
-            self.got(index, None, slot)
-            self.put(index, half, self.shard(-da, 0), 2 + slot)
-            self.to_b(da)
+        self.pass_both(self.shard(-1, 0), self.shard(1, 0), self.shard(1, 0), self.shard(-1, 0), 0)
+        self.got(self.shard(-1, 0), 1, 36)
+        self.to_b(-1)
+        self.got(self.shard(1, 0), 0, 37)
+        self.to_b(1)
 
     def end_a(self):
         index = self.shard(2, 0)
@@ -227,12 +237,12 @@
         self.to_b(2)
 
     def pass_b(self, da):
-        base = 4 + 4 * (da + 1)
-        for db, half, slot in ((-1, 0, 0), (1, 1, 1)):
-            index = self.shard(da, db)
-            self.got(index, None, base + slot)
-            self.put(index, half, self.shard(0, -db), base + 2 + slot)
-            self.put(index, None, self.sibling, 20 + 4 * (da + 1) + db + 1)
+        lower, upper, slot = self.shard(da, -1), self.shard(da, 1), 36 + 2 * (da + 2)
+        self.pass_both(lower, upper, self.shard(0, 1), self.shard(0, -1), 4 + 4 * (da + 1))
+        self.got(lower, 1, slot)
+        self.put(lower, None, self.sibling, 20 + 4 * (da + 1))
+        self.got(upper, 0, slot + 1)
+        self.put(upper, None, self.sibling, 20 + 4 * (da + 1) + 2)
 
     def end_b(self, da):
         base = 4 + 4 * (da + 1)
@@ -262,11 +272,11 @@
 
 
 def whole_kernel(
-    audio_in, starts, lengths, slots, conv1_in, conv2_in, proj_in, qkv_in, out_in,
+    audio_in, starts_in, lengths_in, slots_in, conv1_in, conv2_in, proj_in, qkv_in, out_in,
     dft_high_in, dft_low_in, mel_high_in, mel_low_in, patch_in,
     regrouped, attended,
     ext, frames_high, frames_low, log_mel, patches, taps, first, features,
-    conv2, dft_high, dft_low, mel_high, mel_low, patch_map,
+    starts, lengths, slots, conv1, conv2, dft_high, dft_low, mel_high, mel_low, patch_map,
     proj, wide, rows_out, rows_own, rows_all, mixed, context_out, context_in,
     local_sem, halo_sem, proj_send, proj_recv, wide_send, wide_recv,
     row_send, row_recv, z_send, z_recv, pass_send, pass_recv, keep_sem, context_send, context_recv,
@@ -315,6 +325,12 @@
         for third in range(3)
     ]
 
+    small = [
+        local(source, target, 13 + index)
+        for index, (source, target) in enumerate(
+            ((conv1_in, conv1), (starts_in, starts), (lengths_in, lengths), (slots_in, slots))
+        )
+    ]
     barrier = pltpu.get_barrier_semaphore()
 
     @pl.loop(1, 32)
@@ -338,7 +354,9 @@
         pl.semaphore_signal(
             barrier, inc=1, device_id={"dp": other // 4, "seq": other % 4}, device_id_type=MESH_ID
         )
-    spread_taps(conv1_in, taps)
+    for load in small:
+        load.wait()
+    spread_taps(conv1, taps)
     first[:, :CH] = jnp.zeros((544, CH), BF)
     ext[:, RIM + SPAN :] = jnp.zeros((ROWS, EXT - RIM - SPAN), F32)
     pl.semaphore_wait(barrier, 39)
@@ -365,6 +383,8 @@
     tables = (dft_high, dft_low, mel_high, mel_low)
 
     for q in range(4):
+        if q == 1:
+            ring.to_b(0, True)
         log_mel[q, 64:, :] = mel_of(frames_high[q, 64:, :], frames_low[q, 64:, :], *tables)
 
     loads[5].wait()
@@ -382,8 +402,8 @@
             for i in range(4):
                 conv2_step(group * 4 + i, first, conv2, features)
 
+    ring.pass_a()
     conv1_run(True)
-    ring.pass_a()
     ring.pass_b(0)
     halo.wait_recv()
 
@@ -418,6 +438,7 @@
         part.wait()
     wide_ring = Ring(wide.at[me], wide, wide_send, wide_recv, place)
     wide_ring.begin()
+    wide_ring.to_b(0, True)
     tile_map = jnp.where(
         lax.broadcasted_iota(jnp.int32, (32, 256), 1) % 32 == lax.broadcasted_iota(jnp.int32, (32, 256), 0),
         1.0, 0.0,
@@ -710,16 +731,13 @@
         conv1_weight, conv2_weight, proj_weight, qkv_weight, out_weight.T,
         *spectrum_tables(), *filter_tables(), patch_table(),
     )
-    vmem, anywhere = pl.BlockSpec(memory_space=pltpu.VMEM), pl.BlockSpec(memory_space=pl.ANY)
+    vmem = pl.BlockSpec(memory_space=pltpu.VMEM)
     dma = pltpu.SemaphoreType.DMA
     shape = jax.ShapeDtypeStruct((32, 8, D), BF)
     regrouped, attended = pl.pallas_call(
         whole_kernel,
         out_shape=(shape, shape),
-        in_specs=[
-            anywhere, vmem, vmem, vmem, vmem, anywhere, anywhere, anywhere, anywhere,
-            anywhere, anywhere, anywhere, anywhere, anywhere,
-        ],
+        in_specs=[pl.BlockSpec(memory_space=pltpu.HBM)] * 14,
         out_specs=(vmem, vmem),
         scratch_shapes=[
             pltpu.VMEM((ROWS, EXT), F32),
@@ -730,6 +748,10 @@
             pltpu.VMEM((8, 128, CH), BF),
             pltpu.VMEM((544, 41 * CH), BF),
             pltpu.VMEM((256, 20 * CH), BF),
+            pltpu.VMEM((1, 32), jnp.int32),
+            pltpu.VMEM((1, 32), jnp.int32),
+            pltpu.VMEM((1, 32), jnp.int32),
+            pltpu.VMEM((9, CH), BF),
             pltpu.VMEM((9 * CH, CH), BF),
             pltpu.VMEM((N_FFT, N_FFT), BF),
             pltpu.VMEM((N_FFT, N_FFT), BF),
@@ -744,8 +766,8 @@
             pltpu.VMEM((1024, 3 * PART), BF),
             pltpu.VMEM((4, 256, PART), BF),
             pltpu.VMEM((4, 256, PART), BF),
-            dma((13,)), dma((2,)),
-            dma((36,)), dma((36,)), dma((36,)), dma((36,)),
+            dma((17,)), dma((2,)),
+            dma((46,)), dma((46,)), dma((46,)), dma((46,)),
             dma((32,)), dma((32,)), dma((12,)), dma((12,)), dma((16,)), dma((16,)), dma((4,)), dma((4,)), dma((4,)),
         ],
         compiler_params=pltpu.CompilerParams(

time: 87.2 us -> 85.5 us (0.981)
  Pallas kernels: 83.7 us -> 82 us
    pallas_call x1, Pallas kernels: 83.7 us -> 82 us  [on_device(): pl.pallas_call(whole_kernel, out_shape=(shape, shape), in_specs=[pl.Block...]
where the time goes in v4:
time: 85.5 us; the launch traced here: 85.3 us
  Pallas kernels  82 us (96%)
  local copies, waits for them, and re-layouts  2.72 us (3%)
    pallas_call x1, Pallas kernels, on_device(): pl.pallas_call(whole_kernel, out_shape=(shape, shape), in_specs=[pl.Block...  82 us
    unnamed x4, local copies, waits for them, and re-layouts  2.72 us

profile of v4, /device:TPU:1, one launch (start us, length us, event | category | flops | bytes accessed | tf_op | source)
XLA Modules:
  0.0 85.3 jit_solution(329484323425975448)
XLA Ops:
  0.6 82.0 %whole.1 = (bf16[32,8,1024]{2,1,0:T(8,128)(2,1)}, bf16[32,8,1024]{2,1,0:T(8,128)(2,1)}) custom-call(f32[32,5120]{1,0:T(8,128)} %audio_in.1, s32[1,32]{1,0:T(1,128)} %bitcast.13, s32[1,32]{1,0:T(1,128)} %bitcast.14, s32[1,32]{1,0:T(1,128)} %bitcast.15, bf16[9,256]{1,0:T(8,128)(2,1)} %conv1_in.1, bf16[2304,256]{1,0:T(8,128)(2,1)} %conv2_in.1, ...), custom_call_target="tpu_custom_call" | custom-call | tf_op jit(solution)/shard_map/whole/pallas_call | solution.py:737
  82.6 0.0 copy-start
  82.6 1.9 %copy.20 = bf16[1,32,1,8,1024]{4,3,2,1,0:T(8,128)(2,1)} copy(bf16[1,32,1,8,1024]{4,3,2,1,0:T(8,128)(2,1)} %bitcast.11) | data formatting | bytes 1048576
  84.6 0.0 copy-done
  84.6 0.8 copy.21
Async XLA Ops:
  82.6 1.9 %copy-start = (bf16[32,8,1024]{2,1,0:T(8,128)(2,1)S(1)}, bf16[32,8,1024]{2,1,0:T(8,128)(2,1)}, u32[]{:S(2)}) copy-start(bf16[32,8,1024]{2,1,0:T(8,128)(2,1)} %get-tuple-element.5) | copy-start | bytes 1572868

commit v5 on v4

--- a/solution.py
+++ b/solution.py
@@ -277,7 +277,7 @@
     regrouped, attended,
     ext, frames_high, frames_low, log_mel, patches, taps, first, features,
     starts, lengths, slots, conv1, conv2, dft_high, dft_low, mel_high, mel_low, patch_map,
-    proj, wide, rows_out, rows_own, rows_all, mixed, context_out, context_in,
+    proj, wide, rows_out, rows_own, rows_all, normed, mixed, context_out, context_in,
     local_sem, halo_sem, proj_send, proj_recv, wide_send, wide_recv,
     row_send, row_recv, z_send, z_recv, pass_send, pass_recv, keep_sem, context_send, context_recv,
 ):
@@ -564,6 +564,16 @@
         def _():
             to_sibling(arrived(3, index, 8), 3, index).start()
 
+    def helped(place):
+        @pl.when(helper)
+        def _():
+            for index in range(4):
+                to_sibling(row_part(origins[place], index), place, index).wait_recv()
+
+    def norm(origin):
+        rows = pl.ds(pl.multiple_of(origin * 256, 256), 256)
+        normed[rows, :] = normalised(rows_all[origin].astype(F32).reshape(256, D))
+
     pass_cross(0)
     wide_ring.end_a()
     pass_cross(1)
@@ -576,44 +586,33 @@
     pass_partner(2)
     wide_ring.pass_b(1)
     pass_partner(3)
+
+    @pl.when(keeper)
+    def _():
+        for index in range(4):
+            own_copy(index).wait()
+
+    helped(0)
+    norm(z)
     wide_ring.pass_b(2)
     pass_beyond(0)
     wide_ring.end_b(-1)
     wide_ring.end_b(1)
     pass_beyond(1)
+    helped(1)
+    norm(partner)
+    pass_beyond(2)
     wide_ring.end_b(2)
+    helped(2)
+    norm(cross)
+    pass_beyond(3)
     wide_ring.from_sibling()
-
-    @pl.when(keeper)
-    def _():
-        for index in range(4):
-            own_copy(index).wait()
-
-    def helped(place):
-        @pl.when(helper)
-        def _():
-            for index in range(4):
-                to_sibling(row_part(origins[place], index), place, index).wait_recv()
-
-    def mix(origin):
-        values = rows_all[origin].astype(F32).reshape(256, D)
-        normed = normalised(values)
-        rows = pl.ds(pl.multiple_of(origin * 256, 256), 256)
-        for third in range(3):
-            lanes = pl.ds(pl.multiple_of(third * PAIR + core * PART, 128), PART)
-            result = mm(normed, wide[:, :, lanes].reshape(D, PART))
-            mixed[rows, third * PART : third * PART + PART] = result.astype(BF)
-
-    helped(0)
-    mix(z)
-    pass_beyond(2)
-    helped(1)
-    mix(partner)
-    helped(2)
-    mix(cross)
-    pass_beyond(3)
     helped(3)
-    mix(beyond)
+    norm(beyond)
+    for third in range(3):
+        lanes = pl.ds(pl.multiple_of(third * PAIR + core * PART, 128), PART)
+        result = mm(normed[...], wide[:, :, lanes].reshape(D, PART))
+        mixed[:, third * PART : third * PART + PART] = result.astype(BF)
 
     def bounds(owner):
         chosen = slots[...] == owner
@@ -763,6 +762,7 @@
             pltpu.VMEM((32, 8, D), BF),
             pltpu.VMEM((32, 8, D), BF),
             pltpu.VMEM((4, 32, 8, D), BF),
+            pltpu.VMEM((1024, D), BF),
             pltpu.VMEM((1024, 3 * PART), BF),
             pltpu.VMEM((4, 256, PART), BF),
             pltpu.VMEM((4, 256, PART), BF),

time: 85.5 us -> 84.2 us (0.985)
  Pallas kernels: 82 us -> 80.7 us
    pallas_call x1, Pallas kernels: 82 us -> 80.7 us  [on_device(): pl.pallas_call(whole_kernel, out_shape=(shape, shape), in_specs=[pl.Block...]
where the time goes in v5:
time: 84.2 us; the launch traced here: 84.1 us
  Pallas kernels  80.7 us (96%)
  local copies, waits for them, and re-layouts  2.72 us (3%)
    pallas_call x1, Pallas kernels, on_device(): pl.pallas_call(whole_kernel, out_shape=(shape, shape), in_specs=[pl.Block...  80.7 us
    unnamed x4, local copies, waits for them, and re-layouts  2.72 us

profile of v5, /device:TPU:1, one launch (start us, length us, event | category | flops | bytes accessed | tf_op | source)
XLA Modules:
  0.0 84.1 jit_solution(2066092467679859226)
XLA Ops:
  0.6 80.7 %whole.1 = (bf16[32,8,1024]{2,1,0:T(8,128)(2,1)}, bf16[32,8,1024]{2,1,0:T(8,128)(2,1)}) custom-call(f32[32,5120]{1,0:T(8,128)} %audio_in.1, s32[1,32]{1,0:T(1,128)} %bitcast.13, s32[1,32]{1,0:T(1,128)} %bitcast.14, s32[1,32]{1,0:T(1,128)} %bitcast.15, bf16[9,256]{1,0:T(8,128)(2,1)} %conv1_in.1, bf16[2304,256]{1,0:T(8,128)(2,1)} %conv2_in.1, ...), custom_call_target="tpu_custom_call" | custom-call | tf_op jit(solution)/shard_map/whole/pallas_call | solution.py:736
  81.4 0.0 copy-start
  81.4 1.9 %copy.20 = bf16[1,32,1,8,1024]{4,3,2,1,0:T(8,128)(2,1)} copy(bf16[1,32,1,8,1024]{4,3,2,1,0:T(8,128)(2,1)} %bitcast.11) | data formatting | bytes 1048576
  83.3 0.0 copy-done
  83.3 0.8 copy.21
Async XLA Ops:
  81.4 1.9 %copy-start = (bf16[32,8,1024]{2,1,0:T(8,128)(2,1)S(1)}, bf16[32,8,1024]{2,1,0:T(8,128)(2,1)}, u32[]{:S(2)}) copy-start(bf16[32,8,1024]{2,1,0:T(8,128)(2,1)} %get-tuple-element.5) | copy-start | bytes 1572868

commit v6 on v5

--- a/solution.py
+++ b/solution.py
@@ -451,23 +451,26 @@
     ring.from_sibling()
     loads[7].wait()
 
-    projected = mm(features[...], proj[...].reshape(20 * CH, D)).astype(BF)
-    rows_out[...] = mm(routing, projected).reshape(32, 8, D).astype(BF)
-
-    def row_copy(offset):
+    def row_copy(offset, half):
         target = lax.rem(x + 4 - offset // 8, 4) * 8 + lax.rem(me + offset, 8)
+        lanes = pl.ds(half * 512, 512)
         return pltpu.make_async_remote_copy(
-            src_ref=rows_out.at[target],
-            dst_ref=rows_own.at[me],
-            send_sem=row_send.at[offset],
+            src_ref=rows_out.at[target, :, lanes],
+            dst_ref=rows_own.at[me, :, lanes],
+            send_sem=row_send.at[32 * half + offset],
             recv_sem=row_recv.at[me],
             device_id={"dp": target},
             device_id_type=MESH_ID,
         )
 
-    @pl.loop(1, 32)
-    def _(offset):
-        row_copy(offset).start()
+    for half in range(2):
+        lanes = slice(half * 512, half * 512 + 512)
+        projected = mm(features[...], proj[:, :, lanes].reshape(20 * CH, 512)).astype(BF)
+        rows_out[:, :, lanes] = mm(routing, projected).reshape(32, 8, 512).astype(BF)
+
+        @pl.loop(1, 32)
+        def _(offset):
+            row_copy(offset, half).start()
 
     mine = local(rows_out.at[me], rows_own.at[me], 11)
     wide_ring.pass_a()
@@ -632,12 +635,13 @@
     def context_target(step):
         return lax.rem(z + 2 + step - step // 2 * (2 * step - 1), 4)
 
-    def context_copy(step):
+    def context_copy(step, head):
         target = context_target(step)
+        lanes = pl.ds(head * HEAD_DIM, HEAD_DIM)
         return pltpu.make_async_remote_copy(
-            src_ref=context_out.at[target],
-            dst_ref=context_in.at[pair],
-            send_sem=context_send.at[step],
+            src_ref=context_out.at[target, :, lanes],
+            dst_ref=context_in.at[pair, :, lanes],
+            send_sem=context_send.at[2 * step + head],
             recv_sem=context_recv.at[pair],
             device_id={"dp": row, "seq": target},
             device_id_type=MESH_ID,
@@ -657,17 +661,13 @@
             total = jnp.sum(weights, axis=1, keepdims=True)
             context_out[target, :, lanes] = (mm(weights.astype(BF), value) / total).astype(BF)
 
-        @pl.when(step < 3)
-        def _():
-            context_copy(step).start()
+            @pl.when((step < 3) | helper)
+            def _():
+                context_copy(step, head).start()
 
     @pl.when(keeper)
     def _():
         context_in[pair] = context_out[z]
-
-    @pl.when(helper)
-    def _():
-        context_copy(3).start()
 
     def context_wait(other):
         pltpu.make_async_remote_copy(
@@ -701,7 +701,8 @@
 
     @pl.loop(1, 32)
     def _(offset):
-        row_copy(offset).wait_send()
+        for half in range(2):
+            row_copy(offset, half).wait_send()
 
     @pl.when(keeper)
     def _():
@@ -715,11 +716,13 @@
     def _():
         for index in range(4):
             own_across(index).wait_send()
-        context_copy(3).wait_send()
+        for head in range(2):
+            context_copy(3, head).wait_send()
 
     @pl.loop(0, 3)
     def _(step):
-        context_copy(step).wait_send()
+        for head in range(2):
+            context_copy(step, head).wait_send()
 
 
 def on_device(
@@ -768,7 +771,7 @@
             pltpu.VMEM((4, 256, PART), BF),
             dma((17,)), dma((2,)),
             dma((46,)), dma((46,)), dma((46,)), dma((46,)),
-            dma((32,)), dma((32,)), dma((12,)), dma((12,)), dma((16,)), dma((16,)), dma((4,)), dma((4,)), dma((4,)),
+            dma((64,)), dma((32,)), dma((12,)), dma((12,)), dma((16,)), dma((16,)), dma((4,)), dma((8,)), dma((4,)),
         ],
         compiler_params=pltpu.CompilerParams(
             vmem_limit_bytes=VMEM_LIMIT, collective_id=0, has_side_effects=True

time: 84.2 us -> 83.3 us (0.989)
  Pallas kernels: 80.7 us -> 79.8 us
    pallas_call x1, Pallas kernels: 80.7 us -> 79.8 us  [on_device(): pl.pallas_call(whole_kernel, out_shape=(shape, shape), in_specs=[pl.Block...]
where the time goes in v6:
time: 83.3 us; the launch traced here: 83.2 us
  Pallas kernels  79.8 us (96%)
  local copies, waits for them, and re-layouts  2.72 us (3%)
    pallas_call x1, Pallas kernels, on_device(): pl.pallas_call(whole_kernel, out_shape=(shape, shape), in_specs=[pl.Block...  79.8 us
    unnamed x4, local copies, waits for them, and re-layouts  2.72 us

profile of v6, /device:TPU:1, one launch (start us, length us, event | category | flops | bytes accessed | tf_op | source)
XLA Modules:
  0.0 83.2 jit_solution(14898995834880912998)
XLA Ops:
  0.6 79.8 %whole.1 = (bf16[32,8,1024]{2,1,0:T(8,128)(2,1)}, bf16[32,8,1024]{2,1,0:T(8,128)(2,1)}) custom-call(f32[32,5120]{1,0:T(8,128)} %audio_in.1, s32[1,32]{1,0:T(1,128)} %bitcast.13, s32[1,32]{1,0:T(1,128)} %bitcast.14, s32[1,32]{1,0:T(1,128)} %bitcast.15, bf16[9,256]{1,0:T(8,128)(2,1)} %conv1_in.1, bf16[2304,256]{1,0:T(8,128)(2,1)} %conv2_in.1, ...), custom_call_target="tpu_custom_call" | custom-call | tf_op jit(solution)/shard_map/whole/pallas_call | solution.py:739
  80.4 0.0 copy-start
  80.5 1.9 %copy.20 = bf16[1,32,1,8,1024]{4,3,2,1,0:T(8,128)(2,1)} copy(bf16[1,32,1,8,1024]{4,3,2,1,0:T(8,128)(2,1)} %bitcast.11) | data formatting | bytes 1048576
  82.4 0.0 copy-done
  82.4 0.8 copy.21
Async XLA Ops:
  80.4 1.9 %copy-start = (bf16[32,8,1024]{2,1,0:T(8,128)(2,1)S(1)}, bf16[32,8,1024]{2,1,0:T(8,128)(2,1)}, u32[]{:S(2)}) copy-start(bf16[32,8,1024]{2,1,0:T(8,128)(2,1)} %get-tuple-element.5) | copy-start | bytes 1572868

commit v7 on v6

--- a/solution.py
+++ b/solution.py
@@ -577,6 +577,21 @@
         rows = pl.ds(pl.multiple_of(origin * 256, 256), 256)
         normed[rows, :] = normalised(rows_all[origin].astype(F32).reshape(256, D))
 
+    def bounds(owner):
+        chosen = slots[...] == owner
+        begin = jnp.sum(jnp.where(chosen, starts[...].astype(F32), 0.0), axis=1, keepdims=True)
+        span = jnp.sum(jnp.where(chosen, lengths[...].astype(F32), 0.0), axis=1, keepdims=True)
+        return begin, begin + span
+
+    def valid_of(owner, index, limits):
+        frame = (index // 8 * 4 + owner) * 8 + index % 8
+        sample = (frame * (4 * HOP)).astype(F32)
+        return (sample >= limits[0]) & (sample < limits[1])
+
+    key_index = lax.broadcasted_iota(jnp.int32, (1, 1024), 1)
+    bias = jnp.where(valid_of(key_index // 256, key_index % 256, bounds(row)), 0.0, MASKED)
+    row_valid = valid_of(z, lax.broadcasted_iota(jnp.int32, (256, 1), 0), bounds(me))
+
     pass_cross(0)
     wide_ring.end_a()
     pass_cross(1)
@@ -609,27 +624,14 @@
     helped(2)
     norm(cross)
     pass_beyond(3)
-    wide_ring.from_sibling()
     helped(3)
     norm(beyond)
+    wide_ring.from_sibling()
     for third in range(3):
         lanes = pl.ds(pl.multiple_of(third * PAIR + core * PART, 128), PART)
         result = mm(normed[...], wide[:, :, lanes].reshape(D, PART))
         mixed[:, third * PART : third * PART + PART] = result.astype(BF)
 
-    def bounds(owner):
-        chosen = slots[...] == owner
-        begin = jnp.sum(jnp.where(chosen, starts[...].astype(F32), 0.0), axis=1, keepdims=True)
-        span = jnp.sum(jnp.where(chosen, lengths[...].astype(F32), 0.0), axis=1, keepdims=True)
-        return begin, begin + span
-
-    def valid_of(owner, index, limits):
-        frame = (index // 8 * 4 + owner) * 8 + index % 8
-        sample = (frame * (4 * HOP)).astype(F32)
-        return (sample >= limits[0]) & (sample < limits[1])
-
-    key_index = lax.broadcasted_iota(jnp.int32, (1, 1024), 1)
-    bias = jnp.where(valid_of(key_index // 256, key_index % 256, bounds(row)), 0.0, MASKED)
     scale = HEAD_DIM ** (-0.5) * math.log2(math.e)
 
     def context_target(step):
@@ -690,7 +692,6 @@
     for part in range(4):
         start = 3 * PAIR + part * PART
         output += nt(context_in[part], wide[:, :, start : start + PART].reshape(D, PART))
-    row_valid = valid_of(z, lax.broadcasted_iota(jnp.int32, (256, 1), 0), bounds(me))
     attended[...] = jnp.where(row_valid, output, 0.0).reshape(32, 8, D).astype(BF)
     own = rows_own[...].astype(F32).reshape(256, D)
     regrouped[...] = jnp.where(row_valid, own, 0.0).reshape(32, 8, D).astype(BF)

time: 83.3 us -> 83.4 us (level)
  no operation moved by 1% of the time
where the time goes in v7:
time: 83.4 us; the launch traced here: 83.2 us
  Pallas kernels  79.9 us (96%)
  local copies, waits for them, and re-layouts  2.72 us (3%)
    pallas_call x1, Pallas kernels, on_device(): pl.pallas_call(whole_kernel, out_shape=(shape, shape), in_specs=[pl.Block...  79.9 us
    unnamed x4, local copies, waits for them, and re-layouts  2.72 us

profile of v7, /device:TPU:1, one launch (start us, length us, event | category | flops | bytes accessed | tf_op | source)
XLA Modules:
  0.0 83.2 jit_solution(769307446414311976)
XLA Ops:
  0.6 79.9 %whole.1 = (bf16[32,8,1024]{2,1,0:T(8,128)(2,1)}, bf16[32,8,1024]{2,1,0:T(8,128)(2,1)}) custom-call(f32[32,5120]{1,0:T(8,128)} %audio_in.1, s32[1,32]{1,0:T(1,128)} %bitcast.13, s32[1,32]{1,0:T(1,128)} %bitcast.14, s32[1,32]{1,0:T(1,128)} %bitcast.15, bf16[9,256]{1,0:T(8,128)(2,1)} %conv1_in.1, bf16[2304,256]{1,0:T(8,128)(2,1)} %conv2_in.1, ...), custom_call_target="tpu_custom_call" | custom-call | tf_op jit(solution)/shard_map/whole/pallas_call | solution.py:740
  80.5 0.0 copy-start
  80.5 1.9 %copy.20 = bf16[1,32,1,8,1024]{4,3,2,1,0:T(8,128)(2,1)} copy(bf16[1,32,1,8,1024]{4,3,2,1,0:T(8,128)(2,1)} %bitcast.11) | data formatting | bytes 1048576
  82.4 0.0 copy-done
  82.4 0.8 copy.21
Async XLA Ops:
  80.5 1.9 %copy-start = (bf16[32,8,1024]{2,1,0:T(8,128)(2,1)S(1)}, bf16[32,8,1024]{2,1,0:T(8,128)(2,1)}, u32[]{:S(2)}) copy-start(bf16[32,8,1024]{2,1,0:T(8,128)(2,1)} %get-tuple-element.5) | copy-start | bytes 1572868
